TPU v7x, 256 devices: a whole 4x4x8 slice. The times are simulated.
256 devices in a mesh: mode: 8 (over z_lo, x), space: 32 (over z_hi, y, core).
Axes of the slice: x: 4, y: 4, z: 8 (z_hi: 4, z_lo: 2; z = z_hi * 2 + z_lo), core: 2. Of those that a mesh axis runs over, the one named last changes fastest.
Arguments:
- field: bfloat16 [256, 512, 1024], P('mode', 'space'), may hold values from -6 to 6
- kappa_x: float32 [8, 512, 1024], P(None, 'space'), may hold values from -4 to 4
- kappa_y: float32 [8, 512, 1024], P(None, 'space'), may hold values from -4 to 4
- coupling: bfloat16 [16, 8, 32, 32], P('mode'), may hold values from -0.625 to 0.625
- pattern: int32 [16, 8, 32, 32], P('mode'), may hold values 0 or 1
Outputs:
- image: float32 [256, 512, 1024], P('mode', 'space')
All inputs are finite; a program needn't handle non-finite values. No bound on the sum of `pattern` on one device may be relied on, other than what follows from the above.
Results may differ from a plain program's by a relative error of at most 0.0003.
Values may be sent and summed in bfloat16 or wider, within the bound.
No kernel may reach another device: no remote copies, remote signals or barrier semaphores. Data moves between devices by JAX's collectives and lax.ppermute only.
A program may use at most 64 MiB of HBM per device.

v0:
```python
import jax
import jax.numpy as jnp
from jax import lax
from jax.sharding import PartitionSpec as P


def from_behind(value, axis, steps):
    count = lax.axis_size(axis)
    initial, last = (max(0, -steps), min(count, count - steps))
    return lax.ppermute(value, axis, [(source, source + steps) for source in range(initial, last)])


def passed_along(x, axis, by):
    size = lax.axis_size(axis)
    return lax.ppermute(x, axis, [(i, (i + by) % size) for i in range(size)])


def stacked_mix(tiles, blocks):
    wide = jnp.concatenate(tiles, axis=1)
    tall = jnp.concatenate(blocks, axis=0)
    return jnp.einsum("ij,jrw->irw", wide, tall, preferred_element_type=jnp.float32)


def fluxes(term_of, kappa_x, kappa_y):
    kmodes = kappa_x.shape[0]
    flux_x = None
    flux_y = None
    for k in range(kmodes):
        wk = term_of(k)
        rows = wk.shape[1] - 1
        inner = wk[:, :rows, :]
        diff_x = wk[:, 1:, :] - inner
        next_col = jnp.concatenate(
            [inner[:, :, 1:], jnp.zeros((inner.shape[0], rows, 1), jnp.float32)], axis=2
        )
        part_x = kappa_x[k] * diff_x
        part_y = kappa_y[k] * (next_col - inner)
        flux_x = part_x if flux_x is None else flux_x + part_x
        flux_y = part_y if flux_y is None else flux_y + part_y
    return (flux_x, flux_y)


def divergence(flux_x, flux_y, below):
    prev_x = jnp.concatenate([below, flux_x[:, :-1, :]], axis=1)
    prev_y = jnp.concatenate(
        [jnp.zeros(flux_y.shape[:2] + (1,), jnp.float32), flux_y[:, :, :-1]], axis=2
    )
    return -(flux_x - prev_x) - (flux_y - prev_y)


def shards(field, kappa_x, kappa_y, coupling, pattern):
    coef = jnp.where(pattern > 0, coupling, jnp.zeros(coupling.shape, jnp.bfloat16))
    half = coef[0] * 0.5
    rim = from_behind(field[:, :1, :], "space", -1)
    extended = jnp.concatenate([field, rim], axis=1)
    uppers = []
    lowers = []
    lower_coefs = []
    uppers.append(passed_along(extended, "mode", -1))
    low_block, low_coef = passed_along((extended, coef[1]), "mode", 1)
    lowers.append(low_block)
    lower_coefs.append(low_coef)

    def term_of(k):
        tiles = [half[k], half[k].T]
        blocks = [extended, extended]
        tiles.append(coef[1, k])
        blocks.append(uppers[0])
        tiles.append(lower_coefs[0][k].T)
        blocks.append(lowers[0])
        return stacked_mix(tiles, blocks)

    flux_x, flux_y = fluxes(term_of, kappa_x, kappa_y)
    below = from_behind(flux_x[:, -1:, :], "space", 1)
    image = divergence(flux_x, flux_y, below)
    return image


def solution(mesh):
    placed = (
        P("mode", "space", None),
        P(None, "space", None),
        P(None, "space", None),
        P("mode", None, None, None),
        P("mode", None, None, None),
    )
    return jax.shard_map(
        shards, mesh=mesh, in_specs=placed, out_specs=P("mode", "space", None), check_vma=False
    )
```

profile of v0, /device:TPU:121, one launch (start us, length us, event | category | flops | bytes accessed | tf_op | source)
XLA Modules:
  0.0 104.0 jit_solution(3441568600728787175)
XLA Ops:
  0.0 1.2 %slice.309 = bf16[32,1,1024]{2,1,0:T(2,128)(2,1)S(1)} slice(bf16[32,16,1024]{2,1,0:T(8,128)(2,1)} %param.5), slice={[0:32], [0:1], [0:1024]} | slice | bytes 131072 | tf_op jit(solution)/shard_map/slice | solution.py:54
  1.3 2.6 %collective-permute-start.1 = (bf16[32,1,1024]{2,0,1:T(8,128)(2,1)S(1)}, bf16[32,1,1024]{2,0,1:T(8,128)(2,1)}, u32[]{:S(2)}, u32[]{:S(2)}) collective-permute-start(bf16[32,1,1024]{2,0,1:T(8,128)(2,1)S(1)} %copy.49), channel_id=1, source_target_pairs={{1,0},{2,1},{3,2},{4,3},{5,4},{6,5},{7,6},{8,7},{9,8},{10,9},{11,1... | collective-permute-start | bytes 196616 | tf_op jit(solution)/shard_map/ppermute | solution.py:10
  3.9 1.1 %compare_select_fusion = bf16[2,8,32,32]{3,2,1,0:T(8,128)(2,1)S(1)} fusion(bf16[2,8,32,32]{3,2,1,0:T(8,128)(2,1)} %param.8, s32[2,8,32,32]{3,2,1,0:T(8,128)} %param.9), kind=kLoop, calls=%fused_computation.28 | loop fusion | flops 32768 | bytes 131072 | tf_op jit(solution)/shard_map/jit(_where)/select_n | solution.py:52
  5.0 0.7 copy.35
  5.7 1.2 %collective-permute-start = (bf16[8,32,32]{1,2,0:T(8,128)(2,1)}, bf16[8,32,32]{1,2,0:T(8,128)(2,1)}, u32[]{:S(2)}, u32[]{:S(2)}) collective-permute-start(bf16[8,32,32]{1,2,0:T(8,128)(2,1)} %copy.35), channel_id=1, source_target_pairs={{0,32},{32,64},{64,96},{96,128},{128,160},{160,192},{192,224},{224... | collective-permute-start | bytes 49160 | tf_op jit(solution)/shard_map/ppermute | solution.py:15
  6.9 0.6 constant_dynamic-update-slice_fusion.1
  7.5 0.1 copy.47
  7.6 3.6 %collective-permute-done.1 = bf16[32,1,1024]{2,0,1:T(8,128)(2,1)} collective-permute-done((bf16[32,1,1024]{2,0,1:T(8,128)(2,1)S(1)}, bf16[32,1,1024]{2,0,1:T(8,128)(2,1)}, u32[]{:S(2)}, u32[]{:S(2)}) %collective-permute-start.1) | collective-permute-done | bytes 65568 | tf_op jit(solution)/shard_map/ppermute | solution.py:10
  11.2 0.8 constant_dynamic-update-slice_fusion
  12.0 2.1 %collective-permute-start.2 = (bf16[32,17,1024]{2,0,1:T(8,128)(2,1)S(1)}, bf16[32,17,1024]{2,0,1:T(8,128)(2,1)}, u32[]{:S(2)}, u32[]{:S(2)}) collective-permute-start(bf16[32,17,1024]{2,0,1:T(8,128)(2,1)S(1)} %constant_dynamic-update-slice_fusion), channel_id=1, source_target_pairs={{0,224},{32,0},{64,32},{96,64},{128,96},{160,128},{192,160},{224,1... | collective-permute-start | bytes 3342344 | tf_op jit(solution)/shard_map/ppermute | solution.py:15
  14.2 0.8 slice_bitcast_fusion.8
  15.0 0.8 slice_bitcast_fusion.16
  15.8 0.6 slice_bitcast_fusion.32
  16.4 0.1 copy.36
  16.5 0.1 copy.39
  16.6 0.1 copy.40
  16.7 0.1 copy.41
  16.8 0.1 copy.42
  16.9 0.1 copy.43
  16.9 0.1 copy.44
  17.0 0.7 copy.45
  17.7 0.8 slice_bitcast_fusion.31
  18.6 17.6 %collective-permute-done.2 = bf16[32,17,1024]{2,0,1:T(8,128)(2,1)} collective-permute-done((bf16[32,17,1024]{2,0,1:T(8,128)(2,1)S(1)}, bf16[32,17,1024]{2,0,1:T(8,128)(2,1)}, u32[]{:S(2)}, u32[]{:S(2)}) %collective-permute-start.2) | collective-permute-done | bytes 1114144 | tf_op jit(solution)/shard_map/ppermute | solution.py:15
  36.1 4.4 %collective-permute-done.3 = bf16[32,17,1024]{2,0,1:T(8,128)(2,1)} collective-permute-done((bf16[32,17,1024]{2,0,1:T(8,128)(2,1)S(1)}, bf16[32,17,1024]{2,0,1:T(8,128)(2,1)}, u32[]{:S(2)}, u32[]{:S(2)}) %collective-permute-start.3) | collective-permute-done | bytes 1114144 | tf_op jit(solution)/shard_map/ppermute | solution.py:15
  40.5 2.3 %fusion.17 = f32[32,17,1024]{2,0,1:T(8,128)S(1)} fusion(bf16[32,32]{1,0:T(8,128)(2,1)S(1)} %get-tuple-element.47, bf16[32,32]{1,0:T(8,128)(2,1)S(1)} %get-tuple-element.21, bf16[32,32]{1,0:T(8,128)(2,1)S(1)} %get-tuple-element.32, bf16[32,32]{1,0:T(8,128)(2,1)S(1)} %copy.36, bf16[32,17,1024]{2,0,1:T(8,128)(2,1)} %collective-permute-done.3, ...), kind=kOutput, calls=%fused_computation.64 | convolution fusion | flops 160464896 | bytes 5578752 | tf_op jit(solution)/shard_map/ij,jrw->irw/dot_general | solution.py:21
  42.8 1.9 %slice.349 = f32[32,16,1023]{2,0,1:T(8,128)} slice(f32[32,17,1024]{2,0,1:T(8,128)S(1)} %fusion.17), slice={[0:32], [0:16], [1:1024]} | slice | bytes 4190208 | tf_op jit(solution)/shard_map/slice | solution.py:34
  44.8 2.3 %fusion.24 = f32[32,17,1024]{2,0,1:T(8,128)S(1)} fusion(bf16[32,32]{1,0:T(8,128)(2,1)S(1)} %get-tuple-element.54, bf16[32,32]{1,0:T(8,128)(2,1)S(1)} %get-tuple-element.28, bf16[32,32]{1,0:T(8,128)(2,1)S(1)} %get-tuple-element.33, bf16[32,32]{1,0:T(8,128)(2,1)S(1)} %copy.39, bf16[32,17,1024]{2,0,1:T(8,128)(2,1)} %collective-permute-done.3, ...), kind=kOutput, calls=%fused_computation.72 | convolution fusion | flops 160464896 | bytes 5578752 | tf_op jit(solution)/shard_map/ij,jrw->irw/dot_general | solution.py:21
  47.0 1.9 %slice.350 = f32[32,16,1023]{2,0,1:T(8,128)} slice(f32[32,17,1024]{2,0,1:T(8,128)S(1)} %fusion.24), slice={[0:32], [0:16], [1:1024]} | slice | bytes 4190208 | tf_op jit(solution)/shard_map/slice | solution.py:34
  49.0 2.3 %fusion.31 = f32[32,17,1024]{2,0,1:T(8,128)S(1)} fusion(bf16[32,32]{1,0:T(8,128)(2,1)S(1)} %get-tuple-element.53, bf16[32,32]{1,0:T(8,128)(2,1)S(1)} %get-tuple-element.27, bf16[32,32]{1,0:T(8,128)(2,1)S(1)} %get-tuple-element.34, bf16[32,32]{1,0:T(8,128)(2,1)S(1)} %copy.40, bf16[32,17,1024]{2,0,1:T(8,128)(2,1)} %collective-permute-done.3, ...), kind=kOutput, calls=%fused_computation.80 | convolution fusion | flops 160464896 | bytes 5578752 | tf_op jit(solution)/shard_map/ij,jrw->irw/dot_general | solution.py:21
  51.2 2.0 %slice.351 = f32[32,16,1023]{2,0,1:T(8,128)} slice(f32[32,17,1024]{2,0,1:T(8,128)S(1)} %fusion.31), slice={[0:32], [0:16], [1:1024]} | slice | bytes 4190208 | tf_op jit(solution)/shard_map/slice | solution.py:34
  53.2 2.3 %fusion.38 = f32[32,17,1024]{2,0,1:T(8,128)S(1)} fusion(bf16[32,32]{1,0:T(8,128)(2,1)S(1)} %get-tuple-element.52, bf16[32,32]{1,0:T(8,128)(2,1)S(1)} %get-tuple-element.26, bf16[32,32]{1,0:T(8,128)(2,1)S(1)} %get-tuple-element.35, bf16[32,32]{1,0:T(8,128)(2,1)S(1)} %copy.41, bf16[32,17,1024]{2,0,1:T(8,128)(2,1)} %collective-permute-done.3, ...), kind=kOutput, calls=%fused_computation.88 | convolution fusion | flops 160464896 | bytes 5578752 | tf_op jit(solution)/shard_map/ij,jrw->irw/dot_general | solution.py:21
  55.5 2.0 %slice.352 = f32[32,16,1023]{2,0,1:T(8,128)} slice(f32[32,17,1024]{2,0,1:T(8,128)S(1)} %fusion.38), slice={[0:32], [0:16], [1:1024]} | slice | bytes 4190208 | tf_op jit(solution)/shard_map/slice | solution.py:34
  57.5 2.3 %fusion.45 = f32[32,17,1024]{2,0,1:T(8,128)S(1)} fusion(bf16[32,32]{1,0:T(8,128)(2,1)S(1)} %get-tuple-element.51, bf16[32,32]{1,0:T(8,128)(2,1)S(1)} %get-tuple-element.25, bf16[32,32]{1,0:T(8,128)(2,1)S(1)} %get-tuple-element.36, bf16[32,32]{1,0:T(8,128)(2,1)S(1)} %copy.42, bf16[32,17,1024]{2,0,1:T(8,128)(2,1)} %collective-permute-done.3, ...), kind=kOutput, calls=%fused_computation.96 | convolution fusion | flops 160464896 | bytes 5578752 | tf_op jit(solution)/shard_map/ij,jrw->irw/dot_general | solution.py:21
  59.7 2.0 %slice.353 = f32[32,16,1023]{2,0,1:T(8,128)} slice(f32[32,17,1024]{2,0,1:T(8,128)S(1)} %fusion.45), slice={[0:32], [0:16], [1:1024]} | slice | bytes 4190208 | tf_op jit(solution)/shard_map/slice | solution.py:34
  61.7 2.3 %fusion.52 = f32[32,17,1024]{2,0,1:T(8,128)S(1)} fusion(bf16[32,32]{1,0:T(8,128)(2,1)S(1)} %get-tuple-element.50, bf16[32,32]{1,0:T(8,128)(2,1)S(1)} %get-tuple-element.24, bf16[32,32]{1,0:T(8,128)(2,1)S(1)} %get-tuple-element.37, bf16[32,32]{1,0:T(8,128)(2,1)S(1)} %copy.43, bf16[32,17,1024]{2,0,1:T(8,128)(2,1)} %collective-permute-done.3, ...), kind=kOutput, calls=%fused_computation.104 | convolution fusion | flops 160464896 | bytes 5578752 | tf_op jit(solution)/shard_map/ij,jrw->irw/dot_general | solution.py:21
  64.0 1.9 %slice.354 = f32[32,16,1023]{2,0,1:T(8,128)} slice(f32[32,17,1024]{2,0,1:T(8,128)S(1)} %fusion.52), slice={[0:32], [0:16], [1:1024]} | slice | bytes 4190208 | tf_op jit(solution)/shard_map/slice | solution.py:34
  65.9 2.3 %fusion.59 = f32[32,17,1024]{2,0,1:T(8,128)S(1)} fusion(bf16[32,32]{1,0:T(8,128)(2,1)S(1)} %get-tuple-element.49, bf16[32,32]{1,0:T(8,128)(2,1)S(1)} %get-tuple-element.23, bf16[32,32]{1,0:T(8,128)(2,1)S(1)} %get-tuple-element.38, bf16[32,32]{1,0:T(8,128)(2,1)S(1)} %copy.44, bf16[32,17,1024]{2,0,1:T(8,128)(2,1)} %collective-permute-done.3, ...), kind=kOutput, calls=%fused_computation.112 | convolution fusion | flops 160464896 | bytes 5578752 | tf_op jit(solution)/shard_map/ij,jrw->irw/dot_general | solution.py:21
  68.2 1.9 %slice.355 = f32[32,16,1023]{2,0,1:T(8,128)} slice(f32[32,17,1024]{2,0,1:T(8,128)S(1)} %fusion.59), slice={[0:32], [0:16], [1:1024]} | slice | bytes 4190208 | tf_op jit(solution)/shard_map/slice | solution.py:34
  70.2 2.2 %fusion.66 = f32[32,17,1024]{2,0,1:T(8,128)S(1)} fusion(bf16[32,32]{1,0:T(8,128)(2,1)S(1)} %get-tuple-element.48, bf16[32,32]{1,0:T(8,128)(2,1)S(1)} %copy-done.6, bf16[32,32]{1,0:T(8,128)(2,1)S(1)} %get-tuple-element.39, bf16[32,32]{1,0:T(8,128)(2,1)S(1)} %copy-done.7, bf16[32,17,1024]{2,0,1:T(8,128)(2,1)} %collective-permute-done.3, ...), kind=kOutput, calls=%fused_computation.120 | convolution fusion | flops 160464896 | bytes 5578752 | tf_op jit(solution)/shard_map/ij,jrw->irw/dot_general | solution.py:21
  72.4 1.9 %slice.356 = f32[32,16,1023]{2,0,1:T(8,128)} slice(f32[32,17,1024]{2,0,1:T(8,128)S(1)} %fusion.66), slice={[0:32], [0:16], [1:1024]} | slice | bytes 4190208 | tf_op jit(solution)/shard_map/slice | solution.py:34
  74.3 6.8 %fusion.1 = f32[32,16,1024]{2,0,1:T(8,128)} fusion(f32[32,17,1024]{2,0,1:T(8,128)S(1)} %fusion.66, f32[32,17,1024]{2,0,1:T(8,128)S(1)} %fusion.59, f32[32,17,1024]{2,0,1:T(8,128)S(1)} %fusion.52, f32[32,17,1024]{2,0,1:T(8,128)S(1)} %fusion.45, f32[32,17,1024]{2,0,1:T(8,128)S(1)} %fusion.38, f32[32,17,1024]{2,0,1:T(8,128)S(1)} %fusion.31, ...), kind=kLoop, calls=%fused_computation.3 | loop fusion | flops 12058624 | bytes 36175872 | tf_op jit(solution)/shard_map/add | solution.py:38
  81.1 1.6 %slice.347 = f32[32,1,1024]{2,0,1:T(8,128)} slice(f32[32,16,1024]{2,0,1:T(8,128)} %fusion.1), slice={[0:32], [15:16], [0:1024]} | slice | bytes 262144 | tf_op jit(solution)/shard_map/slice | solution.py:74
  82.7 4.5 %collective-permute-start.4 = (f32[32,1,1024]{2,0,1:T(8,128)}, f32[32,1,1024]{2,0,1:T(8,128)}, u32[]{:S(2)}, u32[]{:S(2)}) collective-permute-start(f32[32,1,1024]{2,0,1:T(8,128)} %slice.347), channel_id=1, source_target_pairs={{0,1},{1,2},{2,3},{3,4},{4,5},{5,6},{6,7},{7,8},{8,9},{9,10},{10,1... | collective-permute-start | bytes 393224 | tf_op jit(solution)/shard_map/ppermute | solution.py:10
  87.2 9.4 %multiply_add_fusion = f32[32,16,1024]{2,0,1:T(8,128)} fusion(f32[32,16,1023]{2,0,1:T(8,128)} %slice.356, f32[32,16,1023]{2,0,1:T(8,128)} %slice.355, f32[32,16,1023]{2,0,1:T(8,128)} %slice.354, f32[32,16,1023]{2,0,1:T(8,128)} %slice.353, f32[32,16,1023]{2,0,1:T(8,128)} %slice.352, f32[32,16,1023]{2,0,1:T(8,128)} %slice.351, f32[32,16,1023]{2,0,1:T(8,128)} %slice.350, ...), kind=kLoop, calls=%fused_computation.27 | loop fusion | flops 12058624 | bytes 36159488 | tf_op jit(solution)/shard_map/add | solution.py:39
  96.6 1.9 %slice.348 = f32[32,15,1024]{2,0,1:T(8,128)S(1)} slice(f32[32,16,1024]{2,0,1:T(8,128)} %fusion.1), slice={[0:32], [0:15], [0:1024]} | slice | bytes 3932160 | tf_op jit(solution)/shard_map/slice | solution.py:44
  98.6 0.2 copy-done
  98.8 2.6 %fusion.16 = f32[32,16,1024]{2,0,1:T(8,128)S(1)} fusion(f32[32,16,1024]{2,0,1:T(8,128)} %fusion.1, f32[32,15,1024]{2,0,1:T(8,128)S(1)} %slice.348, f32[32,1,1024]{2,0,1:T(8,128)} %collective-permute-done.4, f32[32,16,1024]{2,0,1:T(8,128)S(1)} %copy-done, f32[32,16,1023]{2,0,1:T(8,128)S(1)} %bitcast.147), kind=kLoop, calls=%fused_computation.26 | loop fusion | flops 2621440 | bytes 10483712 | tf_op jit(solution)/shard_map/sub | solution.py:48
  101.4 2.5 %copy.46 = f32[32,16,1024]{2,1,0:T(8,128)} copy(f32[32,16,1024]{2,0,1:T(8,128)S(1)} %fusion.16) | data formatting | bytes 4194304 | tf_op jit(solution)/shard_map/sub | solution.py:48
  (22 shorter events, 0.1 us)
Async XLA Ops:
  0.0 6.9 %copy-start.1 = (bf16[32,16,1024]{2,1,0:T(8,128)(2,1)S(1)}, bf16[32,16,1024]{2,1,0:T(8,128)(2,1)}, u32[]{:S(2)}) copy-start(bf16[32,16,1024]{2,1,0:T(8,128)(2,1)} %param.5) | copy-start | bytes 3145732
  0.0 14.2 %copy-start.4 = (f32[8,16,1024]{2,1,0:T(8,128)S(1)}, f32[8,16,1024]{2,1,0:T(8,128)}, u32[]{:S(2)}) copy-start(f32[8,16,1024]{2,1,0:T(8,128)} %param.7) | copy-start | bytes 1572868
  1.3 9.9 %collective-permute-start.1 = (bf16[32,1,1024]{2,0,1:T(8,128)(2,1)S(1)}, bf16[32,1,1024]{2,0,1:T(8,128)(2,1)}, u32[]{:S(2)}, u32[]{:S(2)}) collective-permute-start(bf16[32,1,1024]{2,0,1:T(8,128)(2,1)S(1)} %copy.49), channel_id=1, source_target_pairs={{1,0},{2,1},{3,2},{4,3},{5,4},{6,5},{7,6},{8,7},{9,8},{10,9},{11,1... | collective-permute-start | bytes 196616 | tf_op jit(solution)/shard_map/ppermute | solution.py:10
  4.9 10.1 %copy-start.5 = (f32[8,16,1024]{2,1,0:T(8,128)S(1)}, f32[8,16,1024]{2,1,0:T(8,128)}, u32[]{:S(2)}) copy-start(f32[8,16,1024]{2,1,0:T(8,128)} %param.6) | copy-start | bytes 1572868
  5.7 12.1 %collective-permute-start = (bf16[8,32,32]{1,2,0:T(8,128)(2,1)}, bf16[8,32,32]{1,2,0:T(8,128)(2,1)}, u32[]{:S(2)}, u32[]{:S(2)}) collective-permute-start(bf16[8,32,32]{1,2,0:T(8,128)(2,1)} %copy.35), channel_id=1, source_target_pairs={{0,32},{32,64},{64,96},{96,128},{128,160},{160,192},{192,224},{224... | collective-permute-start | bytes 49160 | tf_op jit(solution)/shard_map/ppermute | solution.py:15
  12.0 53.9 %copy-start.2 = (bf16[32,17,1024]{2,0,1:T(8,128)(2,1)}, bf16[32,17,1024]{2,0,1:T(8,128)(2,1)S(1)}, u32[]{:S(2)}) copy-start(bf16[32,17,1024]{2,0,1:T(8,128)(2,1)S(1)} %constant_dynamic-update-slice_fusion) | copy-start | bytes 3342340
  12.0 24.1 %collective-permute-start.2 = (bf16[32,17,1024]{2,0,1:T(8,128)(2,1)S(1)}, bf16[32,17,1024]{2,0,1:T(8,128)(2,1)}, u32[]{:S(2)}, u32[]{:S(2)}) collective-permute-start(bf16[32,17,1024]{2,0,1:T(8,128)(2,1)S(1)} %constant_dynamic-update-slice_fusion), channel_id=1, source_target_pairs={{0,224},{32,0},{64,32},{96,64},{128,96},{160,128},{192,160},{224,1... | collective-permute-start | bytes 3342344 | tf_op jit(solution)/shard_map/ppermute | solution.py:15
  14.2 26.4 %collective-permute-start.3 = (bf16[32,17,1024]{2,0,1:T(8,128)(2,1)S(1)}, bf16[32,17,1024]{2,0,1:T(8,128)(2,1)}, u32[]{:S(2)}, u32[]{:S(2)}) collective-permute-start(bf16[32,17,1024]{2,0,1:T(8,128)(2,1)S(1)} %constant_dynamic-update-slice_fusion), channel_id=1, source_target_pairs={{0,32},{32,64},{64,96},{96,128},{128,160},{160,192},{192,224},{224... | collective-permute-start | bytes 3342344 | tf_op jit(solution)/shard_map/ppermute | solution.py:15
  68.2 2.0 %copy-start.3 = (bf16[32,17,1024]{2,0,1:T(8,128)(2,1)S(1)}, bf16[32,17,1024]{2,0,1:T(8,128)(2,1)}, u32[]{:S(2)}) copy-start(bf16[32,17,1024]{2,0,1:T(8,128)(2,1)} %copy-done.2) | copy-start | bytes 3342340
  68.2 2.0 %copy-start.6 = (bf16[32,32]{1,0:T(8,128)(2,1)S(1)}, bf16[32,32]{1,0:T(8,128)(2,1)}, u32[]{:S(2)}) copy-start(bf16[32,32]{1,0:T(8,128)(2,1)} %get-tuple-element.22) | copy-start | bytes 6148
  68.2 2.0 %copy-start.7 = (bf16[32,32]{1,0:T(8,128)(2,1)S(1)}, bf16[32,32]{1,0:T(8,128)(2,1)}, u32[]{:S(2)}) copy-start(bf16[32,32]{1,0:T(8,128)(2,1)} %copy.45) | copy-start | bytes 6148
  82.7 15.9 %collective-permute-start.4 = (f32[32,1,1024]{2,0,1:T(8,128)}, f32[32,1,1024]{2,0,1:T(8,128)}, u32[]{:S(2)}, u32[]{:S(2)}) collective-permute-start(f32[32,1,1024]{2,0,1:T(8,128)} %slice.347), channel_id=1, source_target_pairs={{0,1},{1,2},{2,3},{3,4},{4,5},{5,6},{6,7},{7,8},{8,9},{9,10},{10,1... | collective-permute-start | bytes 393224 | tf_op jit(solution)/shard_map/ppermute | solution.py:10
  96.6 2.2 %copy-start = (f32[32,16,1024]{2,0,1:T(8,128)S(1)}, f32[32,16,1024]{2,0,1:T(8,128)}, u32[]{:S(2)}) copy-start(f32[32,16,1024]{2,0,1:T(8,128)} %multiply_add_fusion) | copy-start | bytes 6291460
where the time goes:
time: 105 us; the launch traced here: 104 us
  local copies, waits for them, and re-layouts  29.8 us (28%)
  waiting for transfers between devices  25.6 us (24%)
  other arithmetic  19.9 us (19%)
  matrix products  18.1 us (17%)
  starting transfers between devices  10.4 us (10%)
    ppermute x3, waiting for transfers between devices, passed_along(): return lax.ppermute(x, axis, [(i, (i + by) % size) for i in range(size)])  22 us
    dot_general x8, matrix products, stacked_mix(): jnp.einsum('ij,jrw->irw', wide, tall, preferred_element_type=jnp.float32)  18.1 us
    slice x8, local copies, waits for them, and re-layouts, fluxes(): inner[:, :, 1:]  15.6 us
    add x1, other arithmetic, fluxes(): flux_y = part_y if flux_y is None else flux_y + part_y  9.43 us
    ppermute x2, starting transfers between devices, from_behind(): lax.ppermute(value, axis, [(source, source + steps) for source in range(i...  7.07 us
    add x1, other arithmetic, fluxes(): flux_x = part_x if flux_x is None else flux_x + part_x  6.8 us
    ppermute x2, waiting for transfers between devices, from_behind(): lax.ppermute(value, axis, [(source, source + steps) for source in range(i...  3.58 us
    ppermute x3, starting transfers between devices, passed_along(): return lax.ppermute(x, axis, [(i, (i + by) % size) for i in range(size)])  3.34 us
  transfers between devices with their start and end apart: 5, of which 3 were waited for; matrix products, arithmetic and copies ran while one was open for 18% of the time, Pallas kernels for 0%

commit v1 on v0

v1 whole, which is shorter than its diff:
```python
import functools

import jax
import jax.numpy as jnp
from jax import lax
from jax.experimental import pallas as pl
from jax.experimental.pallas import tpu as pltpu
from jax.sharding import PartitionSpec as P

TILE = 256
HALF = 8


def along_space(x, by):
    count = lax.axis_size("space")
    return lax.ppermute(x, "space", [(i, i + by) for i in range(count) if 0 <= i + by < count])


def along_mode(x, by):
    count = lax.axis_size("mode")
    return lax.ppermute(x, "mode", [(i, (i + by) % count) for i in range(count)])


def vmem_specs(n):
    return [pl.BlockSpec(memory_space=pltpu.VMEM)] * n


def split_body(field_ref, rim_ref, first_ref, second_ref):
    rows = jnp.swapaxes(field_ref[...].astype(jnp.float32), 0, 1).astype(jnp.bfloat16)
    rim_ref[0] = rows[0]
    rim_ref[1] = rows[15]
    first_ref[...] = rows[1:9]
    second_ref[...] = rows[9:15]


def split_rows(field):
    modes, rows, cols = field.shape
    return pl.pallas_call(
        split_body,
        out_shape=(
            jax.ShapeDtypeStruct((2, modes, cols), jnp.bfloat16),
            jax.ShapeDtypeStruct((HALF, modes, cols), jnp.bfloat16),
            jax.ShapeDtypeStruct((rows - HALF - 2, modes, cols), jnp.bfloat16),
        ),
        in_specs=vmem_specs(1),
        out_specs=vmem_specs(3),
        cost_estimate=pl.CostEstimate(flops=0, bytes_accessed=4 * field.size, transcendentals=0),
    )(field)


def image_body(base, mix_ref, kx_ref, ky_ref, kx_rim_ref, *refs):
    groups, (out_ref, stack, behind, sum_p, sum_q, sum_g) = refs[:-6], refs[-6:]
    modes = stack.shape[1] // 4
    cols = stack.shape[2]
    kterms = kx_ref.shape[0]
    place = 0
    for own, upper, lower in zip(groups[0::3], groups[1::3], groups[2::3]):
        n = own.shape[0]
        stack[place : place + n, :modes] = own[...]
        stack[place : place + n, modes : 2 * modes] = own[...]
        stack[place : place + n, 2 * modes : 3 * modes] = upper[...]
        stack[place : place + n, 3 * modes :] = lower[...]
        place += n
    ky = ky_ref[:, base : base + HALF, :]
    lane = lax.broadcasted_iota(jnp.int32, ky.shape, 2)
    behind[...] = jnp.where(lane == 0, 0.0, pltpu.roll(ky, 1, 2))

    def weighted(w, kappa_of):
        total = None
        for k in range(kterms):
            term = kappa_of(k) * w[k * modes : (k + 1) * modes]
            total = term if total is None else total + term
        return total

    def kx_of(i, at):
        if i < 0:
            return lambda k: kx_rim_ref[k : k + 1, at]
        return lambda k: kx_ref[k, i : i + 1, at]

    for n in range(HALF + 2):
        i = base - 1 + n
        for c in range(0, cols, TILE):
            at = slice(c, c + TILE)
            w = jnp.dot(mix_ref[...], stack[n, :, at], preferred_element_type=jnp.float32)
            if n > 0:
                sum_p[n, :, at] = weighted(w, kx_of(i - 1, at))
            if n < HALF + 1:
                sum_q[n, :, at] = weighted(w, kx_of(i, at))
            if 0 < n < HALF + 1:
                ahead = weighted(w, lambda k: behind[k, n - 1 : n, at])
                here = weighted(w, lambda k: ky_ref[k, i : i + 1, at])
                sum_g[0, :, at] = ahead
                sum_g[1, :, at] = here
        if 0 < n < HALF + 1:
            lane = lax.broadcasted_iota(jnp.int32, (modes, cols), 1)
            turned = pltpu.roll(sum_g[1], 1, 1)
            left = sum_g[0] - jnp.where(lane == 0, 0.0, turned)
            ended = jnp.where(lane == 0, -turned, left)
            right = pltpu.roll(ended, cols - 1, 1)
            sum_g[n + 1] = left - right
        if n > 1:
            image = (sum_p[n - 1] - sum_q[n - 2]) - (sum_p[n] - sum_q[n - 1]) + sum_g[n]
            out_ref[:, n - 2, :] = image


def image_rows(base, mix, kappa_x, kappa_y, kx_rim, groups, image):
    modes = groups[0][0].shape[1]
    cols = groups[0][0].shape[2]
    flat = [x for group in groups for x in group]
    rows = kappa_x.shape[1]
    operands = [mix, kappa_x, kappa_y, kx_rim, *flat]
    aliases = {}
    body = functools.partial(image_body, base)
    specs = vmem_specs(len(operands))
    if image is not None:
        aliases = {len(operands): 0}
        operands.append(image)
        specs.append(pl.BlockSpec(memory_space=pl.ANY))
        inner = body
        many = 4 + len(flat)

        def body(*refs):
            inner(*refs[:many], *refs[many + 1 :])

    return pl.pallas_call(
        body,
        grid=(1,),
        out_shape=jax.ShapeDtypeStruct((modes, rows, cols), jnp.float32),
        in_specs=specs,
        out_specs=pl.BlockSpec((modes, HALF, cols), lambda g: (0, base // HALF, 0)),
        scratch_shapes=[
            pltpu.VMEM((HALF + 2, 4 * modes, cols), jnp.bfloat16),
            pltpu.VMEM((kappa_x.shape[0], HALF, cols), jnp.float32),
            pltpu.VMEM((HALF + 2, modes, cols), jnp.float32),
            pltpu.VMEM((HALF + 2, modes, cols), jnp.float32),
            pltpu.VMEM((HALF + 2, modes, cols), jnp.float32),
        ],
        input_output_aliases=aliases,
        compiler_params=pltpu.CompilerParams(vmem_limit_bytes=40 << 20),
        cost_estimate=pl.CostEstimate(
            flops=2 * (HALF + 2) * 8 * modes * 4 * modes * cols, bytes_accessed=8 << 20, transcendentals=0
        ),
    )(*operands)


def shards(field, kappa_x, kappa_y, coupling, pattern):
    kterms, modes = coupling.shape[1], coupling.shape[2]
    rim, first, second = split_rows(field)
    rim_low = along_mode(rim, 1)
    rim_up = along_mode(rim, -1)
    first_low = along_mode(first, 1)
    first_up = along_mode(first, -1)
    coef = jnp.where(pattern > 0, coupling, jnp.zeros(coupling.shape, jnp.bfloat16))
    coef_low = along_mode(coef[1].reshape(kterms, modes * modes), 1).reshape(kterms, modes, modes)
    second_low = along_mode(second, 1)
    second_up = along_mode(second, -1)
    edge = kappa_x.shape[1] - 1
    kx_rim = along_space(kappa_x[:, edge, :], 1)
    top = jnp.concatenate([rim[0], rim_up[0], rim_low[0]], axis=0)
    bottom = jnp.concatenate([rim[1], rim_up[1], rim_low[1]], axis=0)
    after = along_space(top, -1)
    before = along_space(bottom, 1)

    half = coef[0] * 0.5
    mix = jnp.concatenate(
        [half, jnp.swapaxes(half, 1, 2), coef[1], jnp.swapaxes(coef_low, 1, 2)], axis=2
    ).reshape(kterms * modes, 4 * modes)

    def thirds(x):
        return tuple(x[n * modes : (n + 1) * modes][None] for n in range(3))

    image = image_rows(
        0,
        mix,
        kappa_x,
        kappa_y,
        kx_rim,
        [thirds(before), (rim[:1], rim_up[:1], rim_low[:1]), (first, first_up, first_low)],
        None,
    )
    image = image_rows(
        HALF,
        mix,
        kappa_x,
        kappa_y,
        kx_rim,
        [
            (first[6:], first_up[6:], first_low[6:]),
            (second, second_up, second_low),
            (rim[1:], rim_up[1:], rim_low[1:]),
            thirds(after),
        ],
        image,
    )
    return image


def solution(mesh):
    placed = (
        P("mode", "space", None),
        P(None, "space", None),
        P(None, "space", None),
        P("mode", None, None, None),
        P("mode", None, None, None),
    )
    return jax.shard_map(
        shards, mesh=mesh, in_specs=placed, out_specs=P("mode", "space", None), check_vma=False
    )
```

time: 105 us -> 69.2 us (0.66)
  the two profiles are of different devices: /device:TPU:121 before, /device:TPU:160 now
where the time goes in v1:
time: 69.2 us; the launch traced here: 68.8 us
  waiting for transfers between devices  29.7 us (43%)
  starting transfers between devices  18.9 us (27%)
  Pallas kernels  12.6 us (18%)
  local copies, waits for them, and re-layouts  5.45 us (8%)
  other arithmetic  2.06 us (3%)
    ppermute x3, waiting for transfers between devices, along_space(): lax.ppermute(x, 'space', [(i, i + by) for i in range(count) if 0 <= i + b...  25.4 us
    ppermute x7, starting transfers between devices, along_mode(): lax.ppermute(x, 'mode', [(i, (i + by) % count) for i in range(count)])  12.6 us
    pallas_call x2, Pallas kernels, image_rows(): pl.pallas_call(body, grid=(1,), out_shape=jax.ShapeDtypeStruct((modes, ro...  9.94 us
    ppermute x3, starting transfers between devices, along_space(): lax.ppermute(x, 'space', [(i, i + by) for i in range(count) if 0 <= i + b...  6.3 us
    ppermute x7, waiting for transfers between devices, along_mode(): lax.ppermute(x, 'mode', [(i, (i + by) % count) for i in range(count)])  4.26 us
    slice x3, local copies, waits for them, and re-layouts, shards(): top = jnp.concatenate([rim[0], rim_up[0], rim_low[0]], axis=0)  3.37 us
    pallas_call x1, Pallas kernels, split_rows(): pl.pallas_call(split_body, out_shape=(jax.ShapeDtypeStruct((2, modes, col...  2.62 us
  transfers between devices with their start and end apart: 10, of which 4 were waited for; matrix products, arithmetic and copies ran while one was open for 11% of the time, Pallas kernels for 7%

profile of v1, /device:TPU:160, one launch (start us, length us, event | category | flops | bytes accessed | tf_op | source)
XLA Modules:
  0.0 68.8 jit_solution(1461028336318168999)
XLA Ops:
  0.0 0.0 copy-start
  0.0 2.6 %shard_map.55 = (bf16[2,32,1024]{2,1,0:T(8,128)(2,1)}, bf16[8,32,1024]{2,1,0:T(8,128)(2,1)}, bf16[6,32,1024]{2,1,0:T(8,128)(2,1)}) custom-call(bf16[32,16,1024]{2,1,0:T(8,128)(2,1)} %field_ref.1), custom_call_target="tpu_custom_call" | custom-call | bytes 2097152 | tf_op jit(solution)/shard_map/pallas_call | solution.py:38
  2.6 1.5 %collective-permute-start.7 = (bf16[2,32,1024]{2,1,0:T(8,128)(2,1)}, bf16[2,32,1024]{2,1,0:T(8,128)(2,1)}, u32[]{:S(2)}, u32[]{:S(2)}) collective-permute-start(bf16[2,32,1024]{2,1,0:T(8,128)(2,1)} %get-tuple-element.10), channel_id=1, source_target_pairs={{0,32},{32,64},{64,96},{96,128},{128,160},{160,192},{192,224},{224... | collective-permute-start | bytes 393224 | tf_op jit(solution)/shard_map/ppermute | solution.py:21
  4.1 2.6 %collective-permute-start.6 = (bf16[2,32,1024]{2,1,0:T(8,128)(2,1)}, bf16[2,32,1024]{2,1,0:T(8,128)(2,1)}, u32[]{:S(2)}, u32[]{:S(2)}) collective-permute-start(bf16[2,32,1024]{2,1,0:T(8,128)(2,1)} %get-tuple-element.10), channel_id=1, source_target_pairs={{0,224},{32,0},{64,32},{96,64},{128,96},{160,128},{192,160},{224,1... | collective-permute-start | bytes 393224 | tf_op jit(solution)/shard_map/ppermute | solution.py:21
  6.8 0.0 collective-permute-start.5
  6.8 4.1 %collective-permute-start.4 = (bf16[6,32,1024]{2,1,0:T(8,128)(2,1)}, bf16[6,32,1024]{2,1,0:T(8,128)(2,1)S(1)}, u32[]{:S(2)}, u32[]{:S(2)}) collective-permute-start(bf16[6,32,1024]{2,1,0:T(8,128)(2,1)} %get-tuple-element.9.refs_7_), channel_id=1, source_target_pairs={{0,224},{32,0},{64,32},{96,64},{128,96},{160,128},{192,160},{224,1... | collective-permute-start | bytes 1179656 | tf_op jit(solution)/shard_map/ppermute | solution.py:21
  10.9 1.1 %compare_select_fusion = bf16[2,8,32,32]{3,2,1,0:T(8,128)(2,1)S(1)} fusion(bf16[2,8,32,32]{3,2,1,0:T(8,128)(2,1)} %param.8, s32[2,8,32,32]{3,2,1,0:T(8,128)} %param.9), kind=kLoop, calls=%fused_computation | loop fusion | flops 32768 | bytes 131072 | tf_op jit(solution)/shard_map/jit(_where)/select_n | solution.py:153
  12.0 0.1 reshape_squeeze.3
  12.1 0.0 copy-start.1
  12.1 0.0 copy-start.2
  12.1 0.1 collective-permute-start
  12.2 1.6 %fusion.3 = (bf16[1,32,1024]{2,1,0:T(8,128)(2,1)S(1)}, bf16[32,1024]{1,0:T(8,128)(2,1)S(1)}, bf16[32,1024]{1,0:T(8,128)(2,1)}, bf16[1,32,1024]{2,1,0:T(8,128)(2,1)S(1)}) fusion(bf16[2,32,1024]{2,1,0:T(8,128)(2,1)} %get-tuple-element.10), kind=kLoop, calls=%fused_computation.21 | loop fusion | bytes 393216 | tf_op jit(solution)/shard_map/slice | solution.py:159
  13.8 0.0 copy-done
  13.8 0.6 copy.14
  14.5 0.1 copy.9
  14.6 0.9 %slice.64.refs_4_ = bf16[2,32,1024]{2,1,0:T(8,128)(2,1)S(1)} slice(bf16[8,32,1024]{2,1,0:T(8,128)(2,1)} %get-tuple-element.8.refs_6_), slice={[6:8], [0:32], [0:1024]} | slice | bytes 262144 | tf_op jit(solution)/shard_map/slice | solution.py:188
  15.5 4.2 %collective-permute-done = bf16[8,1024]{1,0:T(8,128)(2,1)S(1)} collective-permute-done((bf16[8,1024]{1,0:T(8,128)(2,1)S(1)}, bf16[8,1024]{1,0:T(8,128)(2,1)S(1)}, u32[]{:S(2)}, u32[]{:S(2)}) %collective-permute-start) | collective-permute-done | bytes 16416 | tf_op jit(solution)/shard_map/ppermute | solution.py:21
  19.7 0.0 collective-permute-start.3
  19.7 0.1 reshape.14
  19.8 0.1 copy.10
  19.9 0.0 copy-start.4
  20.0 0.0 collective-permute-done.7
  20.0 4.2 %collective-permute-start.2 = (bf16[8,32,1024]{2,1,0:T(8,128)(2,1)}, bf16[8,32,1024]{2,1,0:T(8,128)(2,1)S(1)}, u32[]{:S(2)}, u32[]{:S(2)}) collective-permute-start(bf16[8,32,1024]{2,1,0:T(8,128)(2,1)} %get-tuple-element.8.refs_6_), channel_id=1, source_target_pairs={{0,224},{32,0},{64,32},{96,64},{128,96},{160,128},{192,160},{224,1... | collective-permute-start | bytes 1572872 | tf_op jit(solution)/shard_map/ppermute | solution.py:21
  24.2 0.9 %fusion.1 = (bf16[1,32,1024]{2,1,0:T(8,128)(2,1)S(1)}, bf16[32,1024]{1,0:T(8,128)(2,1)S(1)}, bf16[32,1024]{1,0:T(8,128)(2,1)S(1)}, bf16[1,32,1024]{2,1,0:T(8,128)(2,1)S(1)}) fusion(bf16[2,32,1024]{2,1,0:T(8,128)(2,1)} %collective-permute-done.7), kind=kLoop, calls=%fused_computation.19 | loop fusion | bytes 393216 | tf_op jit(solution)/shard_map/slice | solution.py:159
  25.1 0.0 collective-permute-done.6
  25.1 0.9 %fusion.2 = (bf16[1,32,1024]{2,1,0:T(8,128)(2,1)S(1)}, bf16[32,1024]{1,0:T(8,128)(2,1)S(1)}, bf16[32,1024]{1,0:T(8,128)(2,1)S(1)}, bf16[1,32,1024]{2,1,0:T(8,128)(2,1)S(1)}) fusion(bf16[2,32,1024]{2,1,0:T(8,128)(2,1)} %collective-permute-done.6), kind=kLoop, calls=%fused_computation.20 | loop fusion | bytes 393216 | tf_op jit(solution)/shard_map/slice | solution.py:159
  26.0 0.9 %pad_maximum_fusion = bf16[96,1024]{1,0:T(8,128)(2,1)S(1)} fusion(bf16[32,1024]{1,0:T(8,128)(2,1)S(1)} %get-tuple-element.19, bf16[32,1024]{1,0:T(8,128)(2,1)S(1)} %get-tuple-element.23, bf16[32,1024]{1,0:T(8,128)(2,1)} %get-tuple-element.27), kind=kLoop, calls=%fused_computation.1 | loop fusion | flops 589824 | bytes 393216 | tf_op jit(solution)/shard_map/concatenate | solution.py:159
  26.8 2.3 %collective-permute-start.8 = (bf16[96,1024]{1,0:T(8,128)(2,1)S(1)}, bf16[96,1024]{1,0:T(8,128)(2,1)S(1)}, u32[]{:S(2)}, u32[]{:S(2)}) collective-permute-start(bf16[96,1024]{1,0:T(8,128)(2,1)S(1)} %pad_maximum_fusion), channel_id=1, source_target_pairs={{1,0},{2,1},{3,2},{4,3},{5,4},{6,5},{7,6},{8,7},{9,8},{10,9},{11,1... | collective-permute-start | bytes 589832 | tf_op jit(solution)/shard_map/ppermute | solution.py:16
  29.2 0.1 pad_maximum_fusion.2.mix_ref.refs_0_
  29.3 8.7 %collective-permute-done.8 = bf16[96,1024]{1,0:T(8,128)(2,1)S(1)} collective-permute-done((bf16[96,1024]{1,0:T(8,128)(2,1)S(1)}, bf16[96,1024]{1,0:T(8,128)(2,1)S(1)}, u32[]{:S(2)}, u32[]{:S(2)}) %collective-permute-start.8) | collective-permute-done | bytes 196640 | tf_op jit(solution)/shard_map/ppermute | solution.py:16
  38.0 1.9 %collective-permute-start.9 = (bf16[96,1024]{1,0:T(8,128)(2,1)S(1)}, bf16[96,1024]{1,0:T(8,128)(2,1)S(1)}, u32[]{:S(2)}, u32[]{:S(2)}) collective-permute-start(bf16[96,1024]{1,0:T(8,128)(2,1)S(1)} %pad_maximum_fusion.1), channel_id=1, source_target_pairs={{0,1},{1,2},{2,3},{3,4},{4,5},{5,6},{6,7},{7,8},{8,9},{9,10},{10,1... | collective-permute-start | bytes 589832 | tf_op jit(solution)/shard_map/ppermute | solution.py:16
  40.0 9.4 %collective-permute-done.9 = bf16[96,1024]{1,0:T(8,128)(2,1)S(1)} collective-permute-done((bf16[96,1024]{1,0:T(8,128)(2,1)S(1)}, bf16[96,1024]{1,0:T(8,128)(2,1)S(1)}, u32[]{:S(2)}, u32[]{:S(2)}) %collective-permute-start.9) | collective-permute-done | bytes 196640 | tf_op jit(solution)/shard_map/ppermute | solution.py:16
  49.4 0.0 copy-done.4
  49.4 2.1 %collective-permute-start.1 = (f32[8,1024]{1,0:T(8,128)S(1)}, f32[8,1024]{1,0:T(8,128)S(1)}, u32[]{:S(2)}, u32[]{:S(2)}) collective-permute-start(f32[8,1024]{1,0:T(8,128)S(1)} %bitcast.43), channel_id=1, source_target_pairs={{0,1},{1,2},{2,3},{3,4},{4,5},{5,6},{6,7},{7,8},{8,9},{9,10},{10,1... | collective-permute-start | bytes 98312 | tf_op jit(solution)/shard_map/ppermute | solution.py:16
  51.5 0.0 collective-permute-done.3.refs_8_
  51.5 0.0 collective-permute-done.2.refs_7_
  51.6 7.3 %collective-permute-done.1.kx_rim_ref.refs_3_ = f32[8,1024]{1,0:T(8,128)S(1)} collective-permute-done((f32[8,1024]{1,0:T(8,128)S(1)}, f32[8,1024]{1,0:T(8,128)S(1)}, u32[]{:S(2)}, u32[]{:S(2)}) %collective-permute-start.1) | collective-permute-done | bytes 32800 | tf_op jit(solution)/shard_map/ppermute | solution.py:16
  58.8 0.0 copy-done.1
  58.8 0.0 copy-done.2
  58.8 0.0 copy-start.3
  58.8 5.0 %shard_map.56.refs_16_ = f32[32,16,1024]{2,1,0:T(8,128)} custom-call(bf16[256,128]{1,0:T(8,128)(2,1)S(1)} %pad_maximum_fusion.2.mix_ref.refs_0_, f32[8,16,1024]{2,1,0:T(8,128)S(1)} %copy-done, f32[8,16,1024]{2,1,0:T(8,128)S(1)} %copy-done.1, f32[8,1024]{1,0:T(8,128)S(1)} %collective-permute-done.1.kx_rim_ref.refs_3_, ...), custom_call_target="tpu_custom_call" | custom-call | flops 671088640 | bytes 8388608 | tf_op jit(solution)/shard_map/pallas_call | solution.py:125
  63.8 0.0 collective-permute-done.5.refs_9_
  63.8 0.0 collective-permute-done.4.refs_8_
  63.8 0.0 copy-done.3
  63.8 5.0 %shard_map.57 = f32[32,16,1024]{2,1,0:T(8,128)} custom-call(bf16[256,128]{1,0:T(8,128)(2,1)S(1)} %pad_maximum_fusion.2.mix_ref.refs_0_, f32[8,16,1024]{2,1,0:T(8,128)S(1)} %copy-done, f32[8,16,1024]{2,1,0:T(8,128)S(1)} %copy-done.1, f32[8,1024]{1,0:T(8,128)S(1)} %collective-permute-done.1.kx_rim_ref.refs_3_, ...), custom_call_target="tpu_custom_call", output_to_operand_aliasing={{}: (16, {})} | custom-call | flops 671088640 | bytes 8388608 | tf_op jit(solution)/shard_map/pallas_call | solution.py:125
  (7 shorter events, 0.1 us)
Async XLA Ops:
  0.0 13.8 %copy-start = (f32[8,16,1024]{2,1,0:T(8,128)S(1)}, f32[8,16,1024]{2,1,0:T(8,128)}, u32[]{:S(2)}) copy-start(f32[8,16,1024]{2,1,0:T(8,128)} %refs_1_.1) | copy-start | bytes 1572868
  2.6 17.3 %collective-permute-start.7 = (bf16[2,32,1024]{2,1,0:T(8,128)(2,1)}, bf16[2,32,1024]{2,1,0:T(8,128)(2,1)}, u32[]{:S(2)}, u32[]{:S(2)}) collective-permute-start(bf16[2,32,1024]{2,1,0:T(8,128)(2,1)} %get-tuple-element.10), channel_id=1, source_target_pairs={{0,32},{32,64},{64,96},{96,128},{128,160},{160,192},{192,224},{224... | collective-permute-start | bytes 393224 | tf_op jit(solution)/shard_map/ppermute | solution.py:21
  4.1 21.0 %collective-permute-start.6 = (bf16[2,32,1024]{2,1,0:T(8,128)(2,1)}, bf16[2,32,1024]{2,1,0:T(8,128)(2,1)}, u32[]{:S(2)}, u32[]{:S(2)}) collective-permute-start(bf16[2,32,1024]{2,1,0:T(8,128)(2,1)} %get-tuple-element.10), channel_id=1, source_target_pairs={{0,224},{32,0},{64,32},{96,64},{128,96},{160,128},{192,160},{224,1... | collective-permute-start | bytes 393224 | tf_op jit(solution)/shard_map/ppermute | solution.py:21
  6.8 57.0 %collective-permute-start.5 = (bf16[6,32,1024]{2,1,0:T(8,128)(2,1)}, bf16[6,32,1024]{2,1,0:T(8,128)(2,1)S(1)}, u32[]{:S(2)}, u32[]{:S(2)}) collective-permute-start(bf16[6,32,1024]{2,1,0:T(8,128)(2,1)} %get-tuple-element.9.refs_7_), channel_id=1, source_target_pairs={{0,32},{32,64},{64,96},{96,128},{128,160},{160,192},{192,224},{224... | collective-permute-start | bytes 1179656 | tf_op jit(solution)/shard_map/ppermute | solution.py:21
  6.8 57.0 %collective-permute-start.4 = (bf16[6,32,1024]{2,1,0:T(8,128)(2,1)}, bf16[6,32,1024]{2,1,0:T(8,128)(2,1)S(1)}, u32[]{:S(2)}, u32[]{:S(2)}) collective-permute-start(bf16[6,32,1024]{2,1,0:T(8,128)(2,1)} %get-tuple-element.9.refs_7_), channel_id=1, source_target_pairs={{0,224},{32,0},{64,32},{96,64},{128,96},{160,128},{192,160},{224,1... | collective-permute-start | bytes 1179656 | tf_op jit(solution)/shard_map/ppermute | solution.py:21
  12.1 46.7 %copy-start.1 = (f32[8,16,1024]{2,1,0:T(8,128)S(1)}, f32[8,16,1024]{2,1,0:T(8,128)}, u32[]{:S(2)}) copy-start(f32[8,16,1024]{2,1,0:T(8,128)} %refs_2_.1) | copy-start | bytes 1572868
  12.1 46.7 %copy-start.2 = (bf16[8,32,1024]{2,1,0:T(8,128)(2,1)S(1)}, bf16[8,32,1024]{2,1,0:T(8,128)(2,1)}, u32[]{:S(2)}) copy-start(bf16[8,32,1024]{2,1,0:T(8,128)(2,1)} %get-tuple-element.8.refs_6_) | copy-start | bytes 1572868
  12.1 7.6 %collective-permute-start = (bf16[8,1024]{1,0:T(8,128)(2,1)S(1)}, bf16[8,1024]{1,0:T(8,128)(2,1)S(1)}, u32[]{:S(2)}, u32[]{:S(2)}) collective-permute-start(bf16[8,1024]{1,0:T(8,128)(2,1)S(1)} %reshape_squeeze.3), channel_id=1, source_target_pairs={{0,32},{32,64},{64,96},{96,128},{128,160},{160,192},{192,224},{224... | collective-permute-start | bytes 49160 | tf_op jit(solution)/shard_map/ppermute | solution.py:21
  19.7 31.8 %collective-permute-start.3 = (bf16[8,32,1024]{2,1,0:T(8,128)(2,1)}, bf16[8,32,1024]{2,1,0:T(8,128)(2,1)S(1)}, u32[]{:S(2)}, u32[]{:S(2)}) collective-permute-start(bf16[8,32,1024]{2,1,0:T(8,128)(2,1)} %get-tuple-element.8.refs_6_), channel_id=1, source_target_pairs={{0,32},{32,64},{64,96},{96,128},{128,160},{160,192},{192,224},{224... | collective-permute-start | bytes 1572872 | tf_op jit(solution)/shard_map/ppermute | solution.py:21
  19.9 29.4 %copy-start.4 = (f32[8,1,1024]{2,0,1:T(8,128)S(1)}, f32[8,1,1024]{2,0,1:T(8,128)}, u32[]{:S(2)}) copy-start(f32[8,1,1024]{2,0,1:T(8,128)} %copy.14) | copy-start | bytes 98308
  20.0 31.6 %collective-permute-start.2 = (bf16[8,32,1024]{2,1,0:T(8,128)(2,1)}, bf16[8,32,1024]{2,1,0:T(8,128)(2,1)S(1)}, u32[]{:S(2)}, u32[]{:S(2)}) collective-permute-start(bf16[8,32,1024]{2,1,0:T(8,128)(2,1)} %get-tuple-element.8.refs_6_), channel_id=1, source_target_pairs={{0,224},{32,0},{64,32},{96,64},{128,96},{160,128},{192,160},{224,1... | collective-permute-start | bytes 1572872 | tf_op jit(solution)/shard_map/ppermute | solution.py:21
  26.8 11.2 %collective-permute-start.8 = (bf16[96,1024]{1,0:T(8,128)(2,1)S(1)}, bf16[96,1024]{1,0:T(8,128)(2,1)S(1)}, u32[]{:S(2)}, u32[]{:S(2)}) collective-permute-start(bf16[96,1024]{1,0:T(8,128)(2,1)S(1)} %pad_maximum_fusion), channel_id=1, source_target_pairs={{1,0},{2,1},{3,2},{4,3},{5,4},{6,5},{7,6},{8,7},{9,8},{10,9},{11,1... | collective-permute-start | bytes 589832 | tf_op jit(solution)/shard_map/ppermute | solution.py:16
  38.0 11.4 %collective-permute-start.9 = (bf16[96,1024]{1,0:T(8,128)(2,1)S(1)}, bf16[96,1024]{1,0:T(8,128)(2,1)S(1)}, u32[]{:S(2)}, u32[]{:S(2)}) collective-permute-start(bf16[96,1024]{1,0:T(8,128)(2,1)S(1)} %pad_maximum_fusion.1), channel_id=1, source_target_pairs={{0,1},{1,2},{2,3},{3,4},{4,5},{5,6},{6,7},{7,8},{8,9},{9,10},{10,1... | collective-permute-start | bytes 589832 | tf_op jit(solution)/shard_map/ppermute | solution.py:16
  49.4 9.4 %collective-permute-start.1 = (f32[8,1024]{1,0:T(8,128)S(1)}, f32[8,1024]{1,0:T(8,128)S(1)}, u32[]{:S(2)}, u32[]{:S(2)}) collective-permute-start(f32[8,1024]{1,0:T(8,128)S(1)} %bitcast.43), channel_id=1, source_target_pairs={{0,1},{1,2},{2,3},{3,4},{4,5},{5,6},{6,7},{7,8},{8,9},{9,10},{10,1... | collective-permute-start | bytes 98312 | tf_op jit(solution)/shard_map/ppermute | solution.py:16
  58.8 5.0 %copy-start.3 = (bf16[6,32,1024]{2,1,0:T(8,128)(2,1)S(1)}, bf16[6,32,1024]{2,1,0:T(8,128)(2,1)}, u32[]{:S(2)}) copy-start(bf16[6,32,1024]{2,1,0:T(8,128)(2,1)} %get-tuple-element.9.refs_7_) | copy-start | bytes 1179652

commit v2 on v0

v2 whole, which is shorter than its diff:
```python
import functools

import jax
import jax.numpy as jnp
from jax import lax
from jax.experimental import pallas as pl
from jax.experimental.pallas import tpu as pltpu
from jax.sharding import PartitionSpec as P

TILE = 256
PIECE = 256
EIGHT = 8
EARLY = 11
FORWARD_COST = 1 << 34
BF16 = jnp.bfloat16
F32 = jnp.float32
ANYWHERE = pl.BlockSpec(memory_space=pl.ANY)
ON_CHIP = pl.BlockSpec(memory_space=pltpu.VMEM)
OFF_CHIP = pl.BlockSpec(memory_space=pltpu.HBM)


def along_space(x, by):
    count = lax.axis_size("space")
    return lax.ppermute(x, "space", [(i, i + by) for i in range(count) if 0 <= i + by < count])


def along_mode(x, by):
    count = lax.axis_size("mode")
    return lax.ppermute(x, "mode", [(i, (i + by) % count) for i in range(count)])


def room(mebibytes):
    return pltpu.CompilerParams(vmem_limit_bytes=mebibytes << 20)


def cost(flops, bytes_accessed):
    return pl.CostEstimate(flops=flops, bytes_accessed=bytes_accessed, transcendentals=0)


def split_body(
    field_hbm,
    coupling_hbm,
    pattern_hbm,
    kx_hbm,
    rim_low,
    rim_up,
    early,
    late,
    edge,
    pieces,
    coupling_ref,
    pattern_ref,
    kx_ref,
    sems,
):
    modes, rows, cols = field_hbm.shape
    wide = pieces.shape[3]
    count = cols // wide
    copies = [
        pltpu.make_async_copy(field_hbm.at[:, :, n * wide : (n + 1) * wide], pieces.at[n], sems.at[n])
        for n in range(count)
    ]
    small = [
        pltpu.make_async_copy(coupling_hbm.at[1], coupling_ref, sems.at[count]),
        pltpu.make_async_copy(pattern_hbm.at[1], pattern_ref, sems.at[count + 1]),
        pltpu.make_async_copy(kx_hbm.at[:, rows - EIGHT :, :], kx_ref, sems.at[count + 2]),
    ]
    for copy in small[:2] + copies + small[2:]:
        copy.start()
    for copy in small[:2]:
        copy.wait()
    coef = jnp.where(pattern_ref[...] > 0, coupling_ref[...].astype(F32), 0.0)
    flat = jnp.concatenate([coef[k] for k in range(coef.shape[0])], axis=1)
    packed = [flat[n * EIGHT : (n + 1) * EIGHT] for n in range(modes // EIGHT)]
    rim_low[2 * modes :] = jnp.concatenate(packed, axis=1).astype(BF16)
    for n, copy in enumerate(copies):
        at = slice(n * wide, (n + 1) * wide)
        copy.wait()
        turned = jnp.swapaxes(pieces[n], 0, 1)
        rim_low[:modes, at] = turned[0]
        rim_low[modes : 2 * modes, at] = turned[rows - 1]
        rim_up[:modes, at] = turned[0]
        rim_up[modes:, at] = turned[rows - 1]
        early[:, :, at] = turned[1 : 1 + EARLY]
        late[:, :, at] = turned[1 + EARLY : rows - 1]
    small[2].wait()
    rest = kx_ref[:, EIGHT - 1, :]
    first = rest.astype(BF16)
    rest = rest - first.astype(F32)
    second = rest.astype(BF16)
    third = (rest - second.astype(F32)).astype(BF16)
    edge[...] = jnp.concatenate([first, second, third, jnp.zeros_like(first)], axis=0)


def split_rows(field, coupling, pattern, kappa_x):
    modes, rows, cols = field.shape
    extra = coupling.shape[1] * modes * modes // cols
    return pl.pallas_call(
        split_body,
        out_shape=(
            jax.ShapeDtypeStruct((2 * modes + extra, cols), BF16),
            jax.ShapeDtypeStruct((2 * modes, cols), BF16),
            jax.ShapeDtypeStruct((EARLY, modes, cols), BF16),
            jax.ShapeDtypeStruct((rows - 2 - EARLY, modes, cols), BF16),
            jax.ShapeDtypeStruct((4 * kappa_x.shape[0], cols), BF16),
        ),
        in_specs=[OFF_CHIP] * 4,
        out_specs=(ON_CHIP,) * 5,
        scratch_shapes=[
            pltpu.VMEM((cols // PIECE, modes, rows, PIECE), BF16),
            pltpu.VMEM(coupling.shape[1:], BF16),
            pltpu.VMEM(pattern.shape[1:], jnp.int32),
            pltpu.VMEM((kappa_x.shape[0], EIGHT, cols), F32),
            pltpu.SemaphoreType.DMA((cols // PIECE + 3,)),
        ],
        compiler_params=room(8),
        cost_estimate=cost(0, 4 * field.size),
    )(*(pltpu.with_memory_space_constraint(x, pltpu.HBM) for x in (field, coupling, pattern, kappa_x)))


def forward_body(own, lower, upper, edge, top, bottom):
    modes = upper.shape[0] // 2
    for n, block in enumerate((own, upper, lower)):
        top[n * modes : (n + 1) * modes] = block[:modes]
        bottom[n * modes : (n + 1) * modes] = block[modes : 2 * modes]
    bottom[3 * modes :] = edge[...]


def forward_rows(own, lower, upper, edge):
    modes, cols = upper.shape[0] // 2, upper.shape[1]
    return pl.pallas_call(
        forward_body,
        out_shape=(
            jax.ShapeDtypeStruct((3 * modes, cols), BF16),
            jax.ShapeDtypeStruct((3 * modes + edge.shape[0], cols), BF16),
        ),
        in_specs=[ON_CHIP] * 4,
        out_specs=(ON_CHIP,) * 2,
        compiler_params=room(4),
        cost_estimate=cost(FORWARD_COST, 1 << 20),
    )(own, lower, upper, edge)


def mix_body(coupling_ref, pattern_ref, lower, mix_ref):
    kterms, modes = coupling_ref.shape[1:3]
    coef = jnp.where(pattern_ref[...] > 0, coupling_ref[...].astype(F32), 0.0)
    half = coef[0] * 0.5
    packed = lower[2 * modes :].astype(F32)
    wide = packed.shape[1] * EIGHT // modes
    low = jnp.concatenate([packed[:, n * wide : (n + 1) * wide] for n in range(modes // EIGHT)], axis=0)
    parts = [half, jnp.swapaxes(half, 1, 2), coef[1]]
    parts = [x.reshape(kterms * modes, modes) for x in parts] + [low.T]
    mix = jnp.concatenate(parts, axis=1)
    mix_ref[...] = jnp.concatenate([-mix, mix], axis=1).astype(BF16)


def mixing(coupling, pattern, lower):
    kterms, modes = coupling.shape[1:3]
    return pl.pallas_call(
        mix_body,
        out_shape=jax.ShapeDtypeStruct((kterms * modes, 8 * modes), BF16),
        in_specs=[ON_CHIP] * 3,
        out_specs=ON_CHIP,
        compiler_params=room(4),
        cost_estimate=cost(0, 1 << 20),
    )(coupling, pattern, lower)


def image_row_values(first, count, kx_of, ky_of, mix_ref, stack, flux, put):
    modes, cols = flux.shape[1:]
    kterms = mix_ref.shape[0] // modes
    depth = stack.shape[1]
    lane = lax.broadcasted_iota(jnp.int32, (modes, cols), 1)
    edge = lax.broadcasted_iota(jnp.int32, (3 * modes, cols), 1) == cols - 1

    def weighted(diff, kappa_of):
        total = None
        for k in range(kterms):
            term = kappa_of(k) * diff[k * modes : (k + 1) * modes]
            total = term if total is None else total + term
        return total

    for n in range(count + 1):
        i = first - 1 + n
        for c in range(0, cols, TILE):
            at = slice(c, c + TILE)
            pair = stack[n : n + 2, :, at].reshape(2 * depth, TILE)
            diff = jnp.dot(mix_ref[...], pair, preferred_element_type=F32)
            flux[n, :, at] = weighted(diff, lambda k: kx_of(i, k, at))
        if n > 0:
            turned = pltpu.roll(stack[n, modes:].astype(F32), cols - 1, 1)
            turned = jnp.where(edge, 0.0, turned).astype(BF16)
            turned = jnp.concatenate([turned[:modes], turned], axis=0)
            across = []
            for c in range(0, cols, TILE):
                at = slice(c, c + TILE)
                pair = jnp.concatenate([stack[n, :, at], turned[:, at]], axis=0)
                diff = jnp.dot(mix_ref[...], pair, preferred_element_type=F32)
                across.append(weighted(diff, lambda k: ky_of(i, k, at)))
            across = jnp.concatenate(across, axis=1)
            left = jnp.where(lane == 0, 0.0, pltpu.roll(across, 1, 1))
            put(i, (flux[n - 1] - flux[n]) + (left - across))


def pile(stack, place, own, upper, lower):
    modes = own.shape[-2]
    stack[place, :modes] = own
    stack[place, modes : 2 * modes] = own
    stack[place, 2 * modes : 3 * modes] = upper
    stack[place, 3 * modes :] = lower


def early_body(mix_ref, kx_ref, ky_ref, before, *refs):
    (own, lower, upper), (inner, inner_low, inner_up), (image, spare, stack, flux, edge_kx) = (
        refs[:3],
        refs[3:6],
        refs[6:],
    )
    modes = upper.shape[0] // 2
    kterms = kx_ref.shape[0]
    pieces = before[3 * modes :].astype(F32)
    edge_kx[...] = (pieces[:kterms] + pieces[kterms : 2 * kterms]) + pieces[2 * kterms : 3 * kterms]
    pile(stack, 0, before[:modes], before[modes : 2 * modes], before[2 * modes : 3 * modes])
    pile(stack, 1, own[:modes], upper[:modes], lower[:modes])
    for n in range(EARLY):
        pile(stack, 2 + n, inner[n], inner_up[n], inner_low[n])

    def put(i, value):
        if i < EIGHT:
            image[:, i, :] = value
        else:
            spare[i - EIGHT] = value

    image_row_values(
        0,
        EARLY,
        lambda i, k, at: edge_kx[k : k + 1, at] if i < 0 else kx_ref[k, i : i + 1, at],
        lambda i, k, at: ky_ref[k, i : i + 1, at],
        mix_ref,
        stack,
        flux,
        put,
    )


def early_image(mix, kappa_x, kappa_y, before, rims, inner):
    kterms, rows, cols = kappa_x.shape
    modes = inner[0].shape[1]
    return pl.pallas_call(
        early_body,
        grid=(1,),
        out_shape=(
            jax.ShapeDtypeStruct((modes, rows, cols), F32),
            jax.ShapeDtypeStruct((EARLY - EIGHT, modes, cols), F32),
        ),
        in_specs=[ON_CHIP] * 10,
        out_specs=(pl.BlockSpec((modes, EIGHT, cols), lambda g: (0, 0, 0)), ON_CHIP),
        scratch_shapes=[
            pltpu.VMEM((EARLY + 2, 4 * modes, cols), BF16),
            pltpu.VMEM((EARLY + 1, modes, cols), F32),
            pltpu.VMEM((kterms, cols), F32),
        ],
        compiler_params=room(20),
        cost_estimate=cost(4 * EARLY * kterms * modes * 8 * modes * cols, 4 << 20),
    )(mix, kappa_x, kappa_y, before, *rims, *inner)


def late_body(mix_ref, kx_ref, ky_ref, after, *refs):
    rims, inner, last, spare, (_, image, stack, flux) = refs[:3], refs[3:6], refs[6:9], refs[9], refs[10:]
    modes = rims[2].shape[0] // 2
    rows = kx_ref.shape[1]
    count = rows - EARLY
    for n in range(EARLY - EIGHT):
        image[:, n, :] = spare[n]
    own, lower, upper = inner
    for n in range(2):
        pile(stack, n, own[EARLY - 2 + n], upper[EARLY - 2 + n], lower[EARLY - 2 + n])
    own, lower, upper = last
    for n in range(count - 2):
        pile(stack, 2 + n, own[n], upper[n], lower[n])
    own, lower, upper = rims
    pile(stack, count, own[modes : 2 * modes], upper[modes:], lower[modes : 2 * modes])
    pile(stack, count + 1, after[:modes], after[modes : 2 * modes], after[2 * modes :])

    def put(i, value):
        image[:, i - EIGHT, :] = value

    image_row_values(
        EARLY,
        count,
        lambda i, k, at: kx_ref[k, i : i + 1, at],
        lambda i, k, at: ky_ref[k, i : i + 1, at],
        mix_ref,
        stack,
        flux,
        put,
    )


def late_image(mix, kappa_x, kappa_y, after, rims, inner, last, spare, image):
    kterms, rows, cols = kappa_x.shape
    modes = inner[0].shape[1]
    count = rows - EARLY
    return pl.pallas_call(
        late_body,
        grid=(1,),
        out_shape=jax.ShapeDtypeStruct((modes, rows, cols), F32),
        in_specs=[ON_CHIP] * 14 + [ANYWHERE],
        out_specs=pl.BlockSpec((modes, EIGHT, cols), lambda g: (0, 1, 0)),
        scratch_shapes=[
            pltpu.VMEM((count + 2, 4 * modes, cols), BF16),
            pltpu.VMEM((count + 1, modes, cols), F32),
        ],
        input_output_aliases={14: 0},
        compiler_params=room(20),
        cost_estimate=cost(4 * count * kterms * modes * 8 * modes * cols, 4 << 20),
    )(mix, kappa_x, kappa_y, after, *rims, *inner, *last, spare, image)


def shards(field, kappa_x, kappa_y, coupling, pattern):
    rim, rim_bare, inner, last, edge = split_rows(field, coupling, pattern, kappa_x)
    rim_low = along_mode(rim, 1)
    rim_up = along_mode(rim_bare, -1)
    inner_low = along_mode(inner, 1)
    inner_up = along_mode(inner, -1)
    top, bottom = forward_rows(rim, rim_low, rim_up, edge)
    before = along_space(bottom, 1)
    after = along_space(top, -1)
    mix = mixing(coupling, pattern, rim_low)
    last_low = along_mode(lax.optimization_barrier((last, top))[0], 1)
    last_up = along_mode(lax.optimization_barrier((last, before))[0], -1)
    rims = (rim, rim_low, rim_up)
    inners = (inner, inner_low, inner_up)
    image, spare = early_image(mix, kappa_x, kappa_y, before, rims, inners)
    return late_image(
        mix, kappa_x, kappa_y, after, rims, inners, (last, last_low, last_up), spare, image
    )


def solution(mesh):
    placed = (
        P("mode", "space", None),
        P(None, "space", None),
        P(None, "space", None),
        P("mode", None, None, None),
        P("mode", None, None, None),
    )
    return jax.shard_map(
        shards, mesh=mesh, in_specs=placed, out_specs=P("mode", "space", None), check_vma=False
    )
```

time: 105 us -> 44.2 us (0.42)
  the two profiles are of different devices: /device:TPU:121 before, /device:TPU:198 now
where the time goes in v2:
time: 44.2 us; the launch traced here: 44 us
  waiting for transfers between devices  19.7 us (45%)
  starting transfers between devices  15 us (34%)
  Pallas kernels  9.15 us (21%)
    ppermute x2, waiting for transfers between devices, along_space(): lax.ppermute(x, 'space', [(i, i + by) for i in range(count) if 0 <= i + b...  12.8 us
    ppermute x2, starting transfers between devices, along_space(): lax.ppermute(x, 'space', [(i, i + by) for i in range(count) if 0 <= i + b...  8.7 us
    ppermute x6, waiting for transfers between devices, along_mode(): lax.ppermute(x, 'mode', [(i, (i + by) % count) for i in range(count)])  6.87 us
    ppermute x6, starting transfers between devices, along_mode(): lax.ppermute(x, 'mode', [(i, (i + by) % count) for i in range(count)])  6.32 us
    pallas_call x1, Pallas kernels, early_image(): pl.pallas_call(early_body, grid=(1,), out_shape=(jax.ShapeDtypeStruct((mo...  4.21 us
    pallas_call x1, Pallas kernels, late_image(): pl.pallas_call(late_body, grid=(1,), out_shape=jax.ShapeDtypeStruct((mode...  3.05 us
    pallas_call x1, Pallas kernels, split_rows(): pl.pallas_call(split_body, out_shape=(jax.ShapeDtypeStruct((2 * modes + e...  1.63 us
  transfers between devices with their start and end apart: 8, of which 3 were waited for; matrix products, arithmetic and copies ran while one was open for 0% of the time, Pallas kernels for 10%

profile of v2, /device:TPU:198, one launch (start us, length us, event | category | flops | bytes accessed | tf_op | source)
XLA Modules:
  0.0 44.0 jit_solution(1819378867924359784)
XLA Ops:
  0.0 1.6 %shard_map.55 = (bf16[72,1024]{1,0:T(8,128)(2,1)S(1)}, bf16[64,1024]{1,0:T(8,128)(2,1)S(1)}, bf16[11,32,1024]{2,1,0:T(8,128)(2,1)S(1)}, bf16[3,32,1024]{2,1,0:T(8,128)(2,1)S(1)}, bf16[32,1024]{1,0:T(8,128)(2,1)S(1)}) custom-call(bf16[32,16,1024]{2,1,0:T(8,128)(2,1)} %field_hbm.1, bf16[2,8,32,32]{3,2,1,0:T(8,128)(2,1)} %coupling_ref.1, ...), custom_call_target="tpu_custom_call" | custom-call | bytes 2097152 | tf_op jit(solution)/shard_map/pallas_call | solution.py:98
  1.6 1.0 %collective-permute-start = (bf16[72,1024]{1,0:T(8,128)(2,1)S(1)}, bf16[72,1024]{1,0:T(8,128)(2,1)S(1)}, u32[]{:S(2)}, u32[]{:S(2)}) collective-permute-start(bf16[72,1024]{1,0:T(8,128)(2,1)S(1)} %get-tuple-element.16.own.refs_0_), channel_id=1, source_target_pairs={{0,32},{32,64},{64,96},{96,128},{128,160},{160,192},{192,224},{224... | collective-permute-start | bytes 442376 | tf_op jit(solution)/shard_map/ppermute | solution.py:29
  2.7 1.1 %collective-permute-start.1 = (bf16[64,1024]{1,0:T(8,128)(2,1)S(1)}, bf16[64,1024]{1,0:T(8,128)(2,1)S(1)}, u32[]{:S(2)}, u32[]{:S(2)}) collective-permute-start(bf16[64,1024]{1,0:T(8,128)(2,1)S(1)} %get-tuple-element.17), channel_id=1, source_target_pairs={{0,224},{32,0},{64,32},{96,64},{128,96},{160,128},{192,160},{224,1... | collective-permute-start | bytes 393224 | tf_op jit(solution)/shard_map/ppermute | solution.py:29
  3.7 0.8 %collective-permute-start.4 = (bf16[11,32,1024]{2,1,0:T(8,128)(2,1)S(1)}, bf16[11,32,1024]{2,1,0:T(8,128)(2,1)S(1)}, u32[]{:S(2)}, u32[]{:S(2)}) collective-permute-start(bf16[11,32,1024]{2,1,0:T(8,128)(2,1)S(1)} %get-tuple-element.20.refs_3_), channel_id=1, source_target_pairs={{0,224},{32,0},{64,32},{96,64},{128,96},{160,128},{192,160},{224,1... | collective-permute-start | bytes 2162696 | tf_op jit(solution)/shard_map/ppermute | solution.py:29
  4.6 3.3 %collective-permute-start.3 = (bf16[11,32,1024]{2,1,0:T(8,128)(2,1)S(1)}, bf16[11,32,1024]{2,1,0:T(8,128)(2,1)S(1)}, u32[]{:S(2)}, u32[]{:S(2)}) collective-permute-start(bf16[11,32,1024]{2,1,0:T(8,128)(2,1)S(1)} %get-tuple-element.20.refs_3_), channel_id=1, source_target_pairs={{0,32},{32,64},{64,96},{96,128},{128,160},{160,192},{192,224},{224... | collective-permute-start | bytes 2162696 | tf_op jit(solution)/shard_map/ppermute | solution.py:29
  7.9 3.3 %collective-permute-done.1.upper.refs_2_ = bf16[64,1024]{1,0:T(8,128)(2,1)S(1)} collective-permute-done((bf16[64,1024]{1,0:T(8,128)(2,1)S(1)}, bf16[64,1024]{1,0:T(8,128)(2,1)S(1)}, u32[]{:S(2)}, u32[]{:S(2)}) %collective-permute-start.1) | collective-permute-done | bytes 131104 | tf_op jit(solution)/shard_map/ppermute | solution.py:29
  11.2 0.0 collective-permute-done.lower.refs_1_
  11.2 0.0 copy-start.1
  11.2 0.0 copy-start.3
  11.2 0.0 copy-start
  11.2 0.0 copy-start.2
  11.3 2.1 %collective-permute-start.6 = (bf16[128,1024]{1,0:T(8,128)(2,1)S(1)}, bf16[128,1024]{1,0:T(8,128)(2,1)S(1)}, u32[]{:S(2)}, u32[]{:S(2)}) collective-permute-start(bf16[128,1024]{1,0:T(8,128)(2,1)S(1)} %get-tuple-element.23), channel_id=1, source_target_pairs={{0,1},{1,2},{2,3},{3,4},{4,5},{5,6},{6,7},{7,8},{8,9},{9,10},{10,1... | collective-permute-start | bytes 786440 | tf_op jit(solution)/shard_map/ppermute | solution.py:24
  13.3 6.7 %collective-permute-start.2 = (bf16[96,1024]{1,0:T(8,128)(2,1)S(1)}, bf16[96,1024]{1,0:T(8,128)(2,1)S(1)}, u32[]{:S(2)}, u32[]{:S(2)}) collective-permute-start(bf16[96,1024]{1,0:T(8,128)(2,1)S(1)} %get-tuple-element.19), channel_id=1, source_target_pairs={{1,0},{2,1},{3,2},{4,3},{5,4},{6,5},{7,6},{8,7},{9,8},{10,9},{11,1... | collective-permute-start | bytes 589832 | tf_op jit(solution)/shard_map/ppermute | solution.py:24
  20.0 0.1 collective-permute-start.5
  20.1 0.0 copy-done.1
  20.1 0.0 copy-done.3
  20.1 0.2 shard_map.56.mix_ref
  20.3 12.8 %collective-permute-done.6.before = bf16[128,1024]{1,0:T(8,128)(2,1)S(1)} collective-permute-done((bf16[128,1024]{1,0:T(8,128)(2,1)S(1)}, bf16[128,1024]{1,0:T(8,128)(2,1)S(1)}, u32[]{:S(2)}, u32[]{:S(2)}) %collective-permute-start.6) | collective-permute-done | bytes 262176 | tf_op jit(solution)/shard_map/ppermute | solution.py:24
  33.2 0.0 collective-permute-start.7
  33.2 0.0 collective-permute-done.4.refs_5_
  33.2 0.0 collective-permute-done.3.refs_4_
  33.2 0.0 copy-done
  33.2 0.0 copy-done.2
  33.2 4.2 %shard_map.58 = (f32[32,16,1024]{2,1,0:T(8,128)}, f32[3,32,1024]{2,1,0:T(8,128)S(1)}) custom-call(bf16[256,256]{1,0:T(8,128)(2,1)S(1)} %shard_map.56.mix_ref, f32[8,16,1024]{2,1,0:T(8,128)S(1)} %copy-done, f32[8,16,1024]{2,1,0:T(8,128)S(1)} %copy-done.2, bf16[128,1024]{1,0:T(8,128)(2,1)S(1)} %collective-permute-done.6.before, ...), custom_call_target="tpu_custom_call" | custom-call | flops 2952790016 | bytes 4194304 | tf_op jit(solution)/shard_map/pallas_call | solution.py:249
  37.4 0.0 collective-permute-done.5.refs_7_
  37.4 0.0 collective-permute-done.2.after
  37.4 3.5 %collective-permute-done.7.refs_8_ = bf16[3,32,1024]{2,1,0:T(8,128)(2,1)S(1)} collective-permute-done((bf16[3,32,1024]{2,1,0:T(8,128)(2,1)S(1)}, bf16[3,32,1024]{2,1,0:T(8,128)(2,1)S(1)}, u32[]{:S(2)}, u32[]{:S(2)}) %collective-permute-start.7) | collective-permute-done | bytes 196640 | tf_op jit(solution)/shard_map/ppermute | solution.py:29
  41.0 3.1 %shard_map.59 = f32[32,16,1024]{2,1,0:T(8,128)} custom-call(bf16[256,256]{1,0:T(8,128)(2,1)S(1)} %shard_map.56.mix_ref, f32[8,16,1024]{2,1,0:T(8,128)S(1)} %copy-done, f32[8,16,1024]{2,1,0:T(8,128)S(1)} %copy-done.2, bf16[96,1024]{1,0:T(8,128)(2,1)S(1)} %collective-permute-done.2.after, ...), custom_call_target="tpu_custom_call", output_to_operand_aliasing={{}: (14, {})} | custom-call | flops 1342177280 | bytes 4194304 | tf_op jit(solution)/shard_map/pallas_call | solution.py:304
  (1 shorter events, 0.0 us)
Async XLA Ops:
  1.6 9.6 %collective-permute-start = (bf16[72,1024]{1,0:T(8,128)(2,1)S(1)}, bf16[72,1024]{1,0:T(8,128)(2,1)S(1)}, u32[]{:S(2)}, u32[]{:S(2)}) collective-permute-start(bf16[72,1024]{1,0:T(8,128)(2,1)S(1)} %get-tuple-element.16.own.refs_0_), channel_id=1, source_target_pairs={{0,32},{32,64},{64,96},{96,128},{128,160},{160,192},{192,224},{224... | collective-permute-start | bytes 442376 | tf_op jit(solution)/shard_map/ppermute | solution.py:29
  2.7 8.6 %collective-permute-start.1 = (bf16[64,1024]{1,0:T(8,128)(2,1)S(1)}, bf16[64,1024]{1,0:T(8,128)(2,1)S(1)}, u32[]{:S(2)}, u32[]{:S(2)}) collective-permute-start(bf16[64,1024]{1,0:T(8,128)(2,1)S(1)} %get-tuple-element.17), channel_id=1, source_target_pairs={{0,224},{32,0},{64,32},{96,64},{128,96},{160,128},{192,160},{224,1... | collective-permute-start | bytes 393224 | tf_op jit(solution)/shard_map/ppermute | solution.py:29
  3.7 29.4 %collective-permute-start.4 = (bf16[11,32,1024]{2,1,0:T(8,128)(2,1)S(1)}, bf16[11,32,1024]{2,1,0:T(8,128)(2,1)S(1)}, u32[]{:S(2)}, u32[]{:S(2)}) collective-permute-start(bf16[11,32,1024]{2,1,0:T(8,128)(2,1)S(1)} %get-tuple-element.20.refs_3_), channel_id=1, source_target_pairs={{0,224},{32,0},{64,32},{96,64},{128,96},{160,128},{192,160},{224,1... | collective-permute-start | bytes 2162696 | tf_op jit(solution)/shard_map/ppermute | solution.py:29
  4.6 28.6 %collective-permute-start.3 = (bf16[11,32,1024]{2,1,0:T(8,128)(2,1)S(1)}, bf16[11,32,1024]{2,1,0:T(8,128)(2,1)S(1)}, u32[]{:S(2)}, u32[]{:S(2)}) collective-permute-start(bf16[11,32,1024]{2,1,0:T(8,128)(2,1)S(1)} %get-tuple-element.20.refs_3_), channel_id=1, source_target_pairs={{0,32},{32,64},{64,96},{96,128},{128,160},{160,192},{192,224},{224... | collective-permute-start | bytes 2162696 | tf_op jit(solution)/shard_map/ppermute | solution.py:29
  11.2 8.9 %copy-start.1 = (s32[2,8,32,32]{3,2,1,0:T(8,128)S(1)}, s32[2,8,32,32]{3,2,1,0:T(8,128)}, u32[]{:S(2)}) copy-start(s32[2,8,32,32]{3,2,1,0:T(8,128)} %pattern_ref.1) | copy-start | bytes 196612
  11.2 8.9 %copy-start.3 = (bf16[2,8,32,32]{3,2,1,0:T(8,128)(2,1)S(1)}, bf16[2,8,32,32]{3,2,1,0:T(8,128)(2,1)}, u32[]{:S(2)}) copy-start(bf16[2,8,32,32]{3,2,1,0:T(8,128)(2,1)} %coupling_ref.1) | copy-start | bytes 98308
  11.2 22.0 %copy-start = (f32[8,16,1024]{2,1,0:T(8,128)S(1)}, f32[8,16,1024]{2,1,0:T(8,128)}, u32[]{:S(2)}) copy-start(f32[8,16,1024]{2,1,0:T(8,128)} %kx_ref.3) | copy-start | bytes 1572868
  11.2 22.0 %copy-start.2 = (f32[8,16,1024]{2,1,0:T(8,128)S(1)}, f32[8,16,1024]{2,1,0:T(8,128)}, u32[]{:S(2)}) copy-start(f32[8,16,1024]{2,1,0:T(8,128)} %ky_ref.3) | copy-start | bytes 1572868
  11.3 21.9 %collective-permute-start.6 = (bf16[128,1024]{1,0:T(8,128)(2,1)S(1)}, bf16[128,1024]{1,0:T(8,128)(2,1)S(1)}, u32[]{:S(2)}, u32[]{:S(2)}) collective-permute-start(bf16[128,1024]{1,0:T(8,128)(2,1)S(1)} %get-tuple-element.23), channel_id=1, source_target_pairs={{0,1},{1,2},{2,3},{3,4},{4,5},{5,6},{6,7},{7,8},{8,9},{9,10},{10,1... | collective-permute-start | bytes 786440 | tf_op jit(solution)/shard_map/ppermute | solution.py:24
  13.3 24.1 %collective-permute-start.2 = (bf16[96,1024]{1,0:T(8,128)(2,1)S(1)}, bf16[96,1024]{1,0:T(8,128)(2,1)S(1)}, u32[]{:S(2)}, u32[]{:S(2)}) collective-permute-start(bf16[96,1024]{1,0:T(8,128)(2,1)S(1)} %get-tuple-element.19), channel_id=1, source_target_pairs={{1,0},{2,1},{3,2},{4,3},{5,4},{6,5},{7,6},{8,7},{9,8},{10,9},{11,1... | collective-permute-start | bytes 589832 | tf_op jit(solution)/shard_map/ppermute | solution.py:24
  20.0 17.4 %collective-permute-start.5 = (bf16[3,32,1024]{2,1,0:T(8,128)(2,1)S(1)}, bf16[3,32,1024]{2,1,0:T(8,128)(2,1)S(1)}, u32[]{:S(2)}, u32[]{:S(2)}) collective-permute-start(bf16[3,32,1024]{2,1,0:T(8,128)(2,1)S(1)} %get-tuple-element.24.refs_6_), channel_id=1, source_target_pairs={{0,32},{32,64},{64,96},{96,128},{128,160},{160,192},{192,224},{224... | collective-permute-start | bytes 589832 | tf_op jit(solution)/shard_map/ppermute | solution.py:29
  33.2 7.8 %collective-permute-start.7 = (bf16[3,32,1024]{2,1,0:T(8,128)(2,1)S(1)}, bf16[3,32,1024]{2,1,0:T(8,128)(2,1)S(1)}, u32[]{:S(2)}, u32[]{:S(2)}) collective-permute-start(bf16[3,32,1024]{2,1,0:T(8,128)(2,1)S(1)} %get-tuple-element.24.refs_6_), channel_id=1, source_target_pairs={{0,224},{32,0},{64,32},{96,64},{128,96},{160,128},{192,160},{224,1... | collective-permute-start | bytes 589832 | tf_op jit(solution)/shard_map/ppermute | solution.py:29

commit v3 on v2

v3 whole, which is shorter than its diff:
```python
import functools

import jax
import jax.numpy as jnp
from jax import lax
from jax.experimental import pallas as pl
from jax.experimental.pallas import tpu as pltpu
from jax.sharding import PartitionSpec as P

TILE = 256
PIECE = 256
EIGHT = 8
KTERMS = 8
EARLY = 11
FORWARD_COST = 1 << 34
BF16 = jnp.bfloat16
F32 = jnp.float32
ANYWHERE = pl.BlockSpec(memory_space=pl.ANY)
ON_CHIP = pl.BlockSpec(memory_space=pltpu.VMEM)
OFF_CHIP = pl.BlockSpec(memory_space=pltpu.HBM)


def swapped(x, axis, first, wraps):
    count = lax.axis_size(axis)
    starts = [i for i in range(first, count, 2) if wraps or i + 1 < count]
    pairs = [(i, (i + 1) % count) for i in starts]
    return lax.ppermute(x, axis, pairs + [(j, i) for i, j in pairs])


def odd_index(axis):
    return lax.rem(lax.axis_index(axis), 2) == 1


def room(mebibytes):
    return pltpu.CompilerParams(vmem_limit_bytes=mebibytes << 20)


def cost(flops, bytes_accessed):
    return pl.CostEstimate(flops=flops, bytes_accessed=bytes_accessed, transcendentals=0)


def split_body(
    field_hbm,
    coupling_hbm,
    pattern_hbm,
    kx_hbm,
    rim,
    early,
    late,
    edge,
    pieces,
    coupling_ref,
    pattern_ref,
    kx_ref,
    sems,
):
    modes, rows, cols = field_hbm.shape
    wide = pieces.shape[3]
    count = cols // wide
    copies = [
        pltpu.make_async_copy(field_hbm.at[:, :, n * wide : (n + 1) * wide], pieces.at[n], sems.at[n])
        for n in range(count)
    ]
    small = [
        pltpu.make_async_copy(coupling_hbm.at[1], coupling_ref, sems.at[count]),
        pltpu.make_async_copy(pattern_hbm.at[1], pattern_ref, sems.at[count + 1]),
        pltpu.make_async_copy(kx_hbm.at[:, rows - EIGHT :, :], kx_ref, sems.at[count + 2]),
    ]
    for copy in small[:2] + copies + small[2:]:
        copy.start()
    for copy in small[:2]:
        copy.wait()
    coef = jnp.where(pattern_ref[...] > 0, coupling_ref[...].astype(F32), 0.0)
    flat = jnp.concatenate([coef[k] for k in range(coef.shape[0])], axis=1)
    packed = [flat[n * EIGHT : (n + 1) * EIGHT] for n in range(modes // EIGHT)]
    rim[2 * modes :] = jnp.concatenate(packed, axis=1).astype(BF16)
    for n, copy in enumerate(copies):
        at = slice(n * wide, (n + 1) * wide)
        copy.wait()
        turned = jnp.swapaxes(pieces[n], 0, 1)
        rim[:modes, at] = turned[0]
        rim[modes : 2 * modes, at] = turned[rows - 1]
        early[:, :, at] = turned[1 : 1 + EARLY]
        late[:, :, at] = turned[1 + EARLY : rows - 1]
    small[2].wait()
    kappa = kx_ref[:, EIGHT - 1, :]
    whole = kappa.astype(BF16)
    edge[...] = jnp.concatenate([whole, (kappa - whole.astype(F32)).astype(BF16)], axis=0)


def split_rows(field, coupling, pattern, kappa_x):
    modes, rows, cols = field.shape
    extra = coupling.shape[1] * modes * modes // cols
    return pl.pallas_call(
        split_body,
        out_shape=(
            jax.ShapeDtypeStruct((2 * modes + extra, cols), BF16),
            jax.ShapeDtypeStruct((EARLY, modes, cols), BF16),
            jax.ShapeDtypeStruct((rows - 2 - EARLY, modes, cols), BF16),
            jax.ShapeDtypeStruct((2 * kappa_x.shape[0], cols), BF16),
        ),
        in_specs=[OFF_CHIP] * 4,
        out_specs=(ON_CHIP,) * 4,
        scratch_shapes=[
            pltpu.VMEM((cols // PIECE, modes, rows, PIECE), BF16),
            pltpu.VMEM(coupling.shape[1:], BF16),
            pltpu.VMEM(pattern.shape[1:], jnp.int32),
            pltpu.VMEM((kappa_x.shape[0], EIGHT, cols), F32),
            pltpu.SemaphoreType.DMA((cols // PIECE + 3,)),
        ],
        compiler_params=room(8),
        cost_estimate=cost(0, 4 * field.size),
    )(*(pltpu.with_memory_space_constraint(x, pltpu.HBM) for x in (field, coupling, pattern, kappa_x)))


def forward_body(own, even, odd, edge, to_even, to_odd):
    modes = to_even.shape[0] // 3 - edge.shape[0] // 3
    flip = odd_index("space")

    def fill(first, last):
        for n, block in enumerate((own, even, odd)):
            at = slice(n * modes, (n + 1) * modes)
            first[at] = block[:modes]
            last[at] = block[modes : 2 * modes]
        first[3 * modes :] = edge[...]
        last[3 * modes :] = edge[...]

    @pl.when(flip)
    def _():
        fill(to_even, to_odd)

    @pl.when(jnp.logical_not(flip))
    def _():
        fill(to_odd, to_even)


def forward_rows(modes, own, even, odd, edge):
    cols = edge.shape[1]
    return pl.pallas_call(
        forward_body,
        out_shape=(jax.ShapeDtypeStruct((3 * modes + edge.shape[0], cols), BF16),) * 2,
        in_specs=[ON_CHIP] * 4,
        out_specs=(ON_CHIP,) * 2,
        compiler_params=room(4),
        cost_estimate=cost(FORWARD_COST, 1 << 20),
    )(own, even, odd, edge)


def mix_body(coupling_ref, pattern_ref, even, odd, mix_ref):
    kterms, modes = coupling_ref.shape[1:3]
    coef = jnp.where(pattern_ref[...] > 0, coupling_ref[...].astype(F32), 0.0)
    half = coef[0] * 0.5
    flip = odd_index("mode")
    packed = jnp.where(flip, even[2 * modes :].astype(F32), odd[2 * modes :].astype(F32))
    wide = packed.shape[1] * EIGHT // modes
    low = jnp.concatenate([packed[:, n * wide : (n + 1) * wide] for n in range(modes // EIGHT)], axis=0).T
    own, turned, up = (
        x.reshape(kterms * modes, modes) for x in (half, jnp.swapaxes(half, 1, 2), coef[1])
    )
    mix = jnp.concatenate([own, turned, jnp.where(flip, low, up), jnp.where(flip, up, low)], axis=1)
    mix_ref[...] = jnp.concatenate([-mix, mix], axis=1).astype(BF16)


def mixing(coupling, pattern, even, odd):
    kterms, modes = coupling.shape[1:3]
    return pl.pallas_call(
        mix_body,
        out_shape=jax.ShapeDtypeStruct((kterms * modes, 8 * modes), BF16),
        in_specs=[ON_CHIP] * 4,
        out_specs=ON_CHIP,
        compiler_params=room(4),
        cost_estimate=cost(0, 1 << 20),
    )(coupling, pattern, even, odd)


def weighted(diff, kappa_of):
    modes = diff.shape[0] // KTERMS
    total = None
    for k in range(KTERMS):
        term = kappa_of(k) * diff[k * modes : (k + 1) * modes]
        total = term if total is None else total + term
    return total


def row_flux(mix_ref, stack, n, at, kappa_of):
    pair = stack[n : n + 2, :, at].reshape(2 * stack.shape[1], at.stop - at.start)
    return weighted(jnp.dot(mix_ref[...], pair, preferred_element_type=F32), kappa_of)


def column_flux(mix_ref, stack, ahead, n, m, at, kappa_of):
    modes = ahead.shape[1] // 3
    pair = jnp.concatenate([stack[n, :, at], ahead[m, :modes, at], ahead[m, :, at]], axis=0)
    return weighted(jnp.dot(mix_ref[...], pair, preferred_element_type=F32), kappa_of)


def pile(stack, place, own, even, odd):
    modes = own.shape[-2]
    stack[place, :modes] = own
    stack[place, modes : 2 * modes] = own
    stack[place, 2 * modes : 3 * modes] = even
    stack[place, 3 * modes :] = odd


def look_ahead(stack, ahead, first, count):
    modes, cols = ahead.shape[1] // 3, ahead.shape[2]
    edge = lax.broadcasted_iota(jnp.int32, (3 * modes, cols), 1) == cols - 1
    for m in range(count):
        turned = pltpu.roll(stack[first + m, modes:], cols - 1, 1)
        ahead[m] = jnp.where(edge, jnp.zeros_like(turned), turned)


def shifted(value, carry):
    lane = lax.broadcasted_iota(jnp.int32, value.shape, 1)
    turned = pltpu.roll(value, 1, 1)
    return jnp.where(lane == 0, carry, turned), turned[:, :1]


def early_body(mix_ref, kx_ref, ky_ref, *refs):
    (own, even, odd), inner, (front, spare, stack, ahead, flux, laid) = refs[:3], refs[3:6], refs[6:]
    modes = front.shape[0]
    cols = front.shape[2]
    pile(stack, 0, own[:modes], even[:modes], odd[:modes])
    for n in range(EARLY):
        pile(stack, 1 + n, *(x[n] for x in inner))
    pile(stack, EARLY + 1, *(x[modes : 2 * modes] for x in (own, even, odd)))
    look_ahead(stack, ahead, 0, EARLY + 2)
    rows = kx_ref.shape[1]
    carry = [jnp.zeros((modes, 1), F32)] * (EARLY + 2)
    for c in range(0, cols, TILE):
        at = slice(c, c + TILE)
        for i in range(EARLY):
            flux[i, :, at] = row_flux(mix_ref, stack, i, at, lambda k: kx_ref[k, i : i + 1, at])
            right = column_flux(mix_ref, stack, ahead, i, i, at, lambda k: ky_ref[k, i : i + 1, at])
            left, carry[i] = shifted(right, carry[i])
            value = (left - right) - flux[i, :, at]
            if i > 0:
                value = value + flux[i - 1, :, at]
            if i < EIGHT:
                laid[i, :, at] = value
            else:
                spare[i - EIGHT, :, at] = value
        front[:, :, at] = jnp.swapaxes(laid[:, :, at], 0, 1)
        spare[EARLY - EIGHT, :, at] = flux[EARLY - 1, :, at]
        for n, i in ((EARLY, EARLY), (EARLY + 1, rows - 1)):
            right = column_flux(mix_ref, stack, ahead, n, n, at, lambda k: ky_ref[k, i : i + 1, at])
            left, carry[n] = shifted(right, carry[n])
            spare[n + 1 - EIGHT, :, at] = left - right


def early_image(mix, kappa_x, kappa_y, rims, inner):
    cols = kappa_x.shape[2]
    modes = inner[0].shape[1]
    return pl.pallas_call(
        early_body,
        out_shape=(
            jax.ShapeDtypeStruct((modes, EIGHT, cols), F32),
            jax.ShapeDtypeStruct((EARLY - EIGHT + 3, modes, cols), F32),
        ),
        in_specs=[ON_CHIP] * 9,
        out_specs=(ON_CHIP, ON_CHIP),
        scratch_shapes=[
            pltpu.VMEM((EARLY + 2, 4 * modes, cols), BF16),
            pltpu.VMEM((EARLY + 2, 3 * modes, cols), BF16),
            pltpu.VMEM((EARLY, modes, cols), F32),
            pltpu.VMEM((EIGHT, modes, cols), F32),
        ],
        compiler_params=room(20),
        cost_estimate=cost(4 * EARLY * KTERMS * modes * 8 * modes * cols, 4 << 20),
    )(mix, kappa_x, kappa_y, *rims, *inner)


def late_body(mix_ref, kx_ref, ky_ref, from_even, from_odd, *refs):
    (own, even, odd), inner, last = refs[:3], refs[3:6], refs[6:9]
    front, spare, image, stack, ahead, edge_kx, laid, out, sems = refs[9:]
    modes = front.shape[0]
    rows, cols = kx_ref.shape[1:]
    count = rows - EARLY
    flip = odd_index("space")

    def either(flipped, at):
        first, second = (from_even, from_odd) if flipped else (from_odd, from_even)
        return jnp.where(flip, first[at].astype(F32), second[at].astype(F32))

    def blocks(flipped):
        return (either(flipped, slice(n * modes, (n + 1) * modes)).astype(BF16) for n in range(3))

    kappa = either(True, slice(3 * modes, None))
    edge_kx[...] = kappa[:KTERMS] + kappa[KTERMS:]
    pile(stack, 0, *blocks(True))
    pile(stack, 1, own[:modes], even[:modes], odd[:modes])
    for c in range(0, cols, TILE):
        at = slice(c, c + TILE)
        above = row_flux(mix_ref, stack, 0, at, lambda k: edge_kx[k : k + 1, at])
        out[0, :, :, at] = front[:, :, at]
        out[0, :, 0, at] = front[:, 0, at] + above
    sends = [pltpu.make_async_copy(out.at[0], image.at[:, :EIGHT, :], sems.at[0])]
    sends[0].start()

    pile(stack, 2, *(x[EARLY - 1] for x in inner))
    for n in range(count - 2):
        pile(stack, 3 + n, *(x[n] for x in last))
    pile(stack, count + 1, *(x[modes : 2 * modes] for x in (own, even, odd)))
    pile(stack, count + 2, *blocks(False))
    look_ahead(stack, ahead, 3, count - 2)
    carry = [jnp.zeros((modes, 1), F32)] * (count - 2)
    for c in range(0, cols, TILE):
        at = slice(c, c + TILE)
        for n in range(EARLY - EIGHT):
            laid[n, :, at] = spare[n, :, at]
        behind = spare[EARLY - EIGHT, :, at]
        for m in range(count):
            i = EARLY + m
            here = row_flux(mix_ref, stack, 2 + m, at, lambda k: kx_ref[k, i : i + 1, at])
            if 0 < m < count - 1:
                right = column_flux(mix_ref, stack, ahead, 2 + m, m - 1, at, lambda k: ky_ref[k, i : i + 1, at])
                left, carry[m - 1] = shifted(right, carry[m - 1])
                across = left - right
            else:
                across = spare[EARLY - EIGHT + 1 + (m > 0), :, at]
            laid[i - EIGHT, :, at] = (behind - here) + across
            behind = here
        out[1, :, :, at] = jnp.swapaxes(laid[:, :, at], 0, 1)
        sends.append(
            pltpu.make_async_copy(out.at[1, :, :, at], image.at[:, EIGHT:, at], sems.at[1 + c // TILE])
        )
        sends[-1].start()
    for send in sends:
        send.wait()


def late_image(mix, kappa_x, kappa_y, from_even, from_odd, rims, inner, last, front, spare):
    kterms, rows, cols = kappa_x.shape
    modes = inner[0].shape[1]
    count = rows - EARLY
    return pl.pallas_call(
        late_body,
        out_shape=jax.ShapeDtypeStruct((modes, rows, cols), F32),
        in_specs=[ON_CHIP] * 16,
        out_specs=OFF_CHIP,
        scratch_shapes=[
            pltpu.VMEM((count + 3, 4 * modes, cols), BF16),
            pltpu.VMEM((count - 2, 3 * modes, cols), BF16),
            pltpu.VMEM((kterms, cols), F32),
            pltpu.VMEM((EIGHT, modes, cols), F32),
            pltpu.VMEM((2, modes, EIGHT, cols), F32),
            pltpu.SemaphoreType.DMA((1 + cols // TILE,)),
        ],
        compiler_params=room(20),
        cost_estimate=cost(4 * count * kterms * modes * 8 * modes * cols, 4 << 20),
    )(mix, kappa_x, kappa_y, from_even, from_odd, *rims, *inner, *last, front, spare)


def shards(field, kappa_x, kappa_y, coupling, pattern):
    rim, inner, last, edge = split_rows(field, coupling, pattern, kappa_x)

    def over_mode(x):
        return x, swapped(x, "mode", 0, True), swapped(x, "mode", 1, True)

    rims = over_mode(rim)
    inners = over_mode(inner)
    to_even, to_odd = forward_rows(field.shape[0], *rims, edge)
    from_even = swapped(to_even, "space", 0, False)
    from_odd = swapped(to_odd, "space", 1, False)
    mix = mixing(coupling, pattern, *rims[1:])
    last = lax.optimization_barrier((last, from_even))[0]
    front, spare = early_image(mix, kappa_x, kappa_y, rims, inners)
    return late_image(
        mix, kappa_x, kappa_y, from_even, from_odd, rims, inners, over_mode(last), front, spare
    )


def solution(mesh):
    placed = (
        P("mode", "space", None),
        P(None, "space", None),
        P(None, "space", None),
        P("mode", None, None, None),
        P("mode", None, None, None),
    )
    return jax.shard_map(
        shards, mesh=mesh, in_specs=placed, out_specs=P("mode", "space", None), check_vma=False
    )
```

time: 44.2 us -> 37.2 us (0.84)
  the two profiles are of different devices: /device:TPU:198 before, /device:TPU:121 now
where the time goes in v3:
time: 37.2 us; the launch traced here: 36.6 us
  starting transfers between devices  14.4 us (39%)
  waiting for transfers between devices  14.1 us (38%)
  Pallas kernels  8.04 us (22%)
    ppermute x8, starting transfers between devices, swapped(): return lax.ppermute(x, axis, pairs + [(j, i) for i, j in pairs])  14.4 us
    ppermute x8, waiting for transfers between devices, swapped(): return lax.ppermute(x, axis, pairs + [(j, i) for i, j in pairs])  14.1 us
    pallas_call x1, Pallas kernels, early_image(): pl.pallas_call(early_body, out_shape=(jax.ShapeDtypeStruct((modes, EIGHT,...  3.71 us
    pallas_call x1, Pallas kernels, late_image(): pl.pallas_call(late_body, out_shape=jax.ShapeDtypeStruct((modes, rows, co...  2.46 us
    pallas_call x1, Pallas kernels, split_rows(): pl.pallas_call(split_body, out_shape=(jax.ShapeDtypeStruct((2 * modes + e...  1.57 us
  transfers between devices with their start and end apart: 8, of which 3 were waited for; matrix products, arithmetic and copies ran while one was open for 0% of the time, Pallas kernels for 11%

profile of v3, /device:TPU:121, one launch (start us, length us, event | category | flops | bytes accessed | tf_op | source)
XLA Modules:
  0.0 36.6 jit_solution(1648749887922408456)
XLA Ops:
  0.0 1.6 %shard_map.55 = (bf16[72,1024]{1,0:T(8,128)(2,1)S(1)}, bf16[11,32,1024]{2,1,0:T(8,128)(2,1)S(1)}, bf16[3,32,1024]{2,1,0:T(8,128)(2,1)S(1)}, bf16[16,1024]{1,0:T(8,128)(2,1)S(1)}) custom-call(bf16[32,16,1024]{2,1,0:T(8,128)(2,1)} %field_hbm.1, bf16[2,8,32,32]{3,2,1,0:T(8,128)(2,1)} %coupling_ref.1, s32[2,8,32,32]{3,2,1,0:T(8,128)} %pattern_ref.1, ...), custom_call_target="tpu_custom_call" | custom-call | bytes 2097152 | tf_op jit(solution)/shard_map/pallas_call | solution.py:94
  1.6 2.1 %collective-permute-start.1 = (bf16[72,1024]{1,0:T(8,128)(2,1)S(1)}, bf16[72,1024]{1,0:T(8,128)(2,1)S(1)}, u32[]{:S(2)}, u32[]{:S(2)}) collective-permute-start(bf16[72,1024]{1,0:T(8,128)(2,1)S(1)} %get-tuple-element.14.own.refs_0_), channel_id=1, source_target_pairs={{32,64},{96,128},{160,192},{224,0},{64,32},{128,96},{192,160},{0,2... | collective-permute-start | bytes 442376 | tf_op jit(solution)/shard_map/ppermute | solution.py:27
  3.7 0.4 %collective-permute-start = (bf16[72,1024]{1,0:T(8,128)(2,1)S(1)}, bf16[72,1024]{1,0:T(8,128)(2,1)S(1)}, u32[]{:S(2)}, u32[]{:S(2)}) collective-permute-start(bf16[72,1024]{1,0:T(8,128)(2,1)S(1)} %get-tuple-element.14.own.refs_0_), channel_id=1, source_target_pairs={{0,32},{64,96},{128,160},{192,224},{32,0},{96,64},{160,128},{224,1... | collective-permute-start | bytes 442376 | tf_op jit(solution)/shard_map/ppermute | solution.py:27
  4.1 1.2 %collective-permute-start.5 = (bf16[11,32,1024]{2,1,0:T(8,128)(2,1)S(1)}, bf16[11,32,1024]{2,1,0:T(8,128)(2,1)S(1)}, u32[]{:S(2)}, u32[]{:S(2)}) collective-permute-start(bf16[11,32,1024]{2,1,0:T(8,128)(2,1)S(1)} %get-tuple-element.18.refs_3_), channel_id=1, source_target_pairs={{32,64},{96,128},{160,192},{224,0},{64,32},{128,96},{192,160},{0,2... | collective-permute-start | bytes 2162696 | tf_op jit(solution)/shard_map/ppermute | solution.py:27
  5.2 0.0 collective-permute-start.4
  5.2 3.2 %collective-permute-done.1.odd.refs_2_ = bf16[72,1024]{1,0:T(8,128)(2,1)S(1)} collective-permute-done((bf16[72,1024]{1,0:T(8,128)(2,1)S(1)}, bf16[72,1024]{1,0:T(8,128)(2,1)S(1)}, u32[]{:S(2)}, u32[]{:S(2)}) %collective-permute-start.1) | collective-permute-done | bytes 147488 | tf_op jit(solution)/shard_map/ppermute | solution.py:27
  8.5 0.0 collective-permute-done.even.refs_1_
  8.5 0.0 copy-start.1
  8.5 0.0 copy-start.3
  8.5 0.0 copy-start
  8.5 0.0 copy-start.2
  8.6 3.0 %collective-permute-start.2 = (bf16[112,1024]{1,0:T(8,128)(2,1)S(1)}, bf16[112,1024]{1,0:T(8,128)(2,1)S(1)}, u32[]{:S(2)}, u32[]{:S(2)}) collective-permute-start(bf16[112,1024]{1,0:T(8,128)(2,1)S(1)} %get-tuple-element.16), channel_id=1, source_target_pairs={{0,1},{2,3},{4,5},{6,7},{8,9},{10,11},{12,13},{14,15},{16,17},{18,... | collective-permute-start | bytes 688136 | tf_op jit(solution)/shard_map/ppermute | solution.py:27
  11.6 5.8 %collective-permute-start.3 = (bf16[112,1024]{1,0:T(8,128)(2,1)S(1)}, bf16[112,1024]{1,0:T(8,128)(2,1)S(1)}, u32[]{:S(2)}, u32[]{:S(2)}) collective-permute-start(bf16[112,1024]{1,0:T(8,128)(2,1)S(1)} %get-tuple-element.17), channel_id=1, source_target_pairs={{1,2},{3,4},{5,6},{7,8},{9,10},{11,12},{13,14},{15,16},{17,18},{19... | collective-permute-start | bytes 688136 | tf_op jit(solution)/shard_map/ppermute | solution.py:27
  17.4 0.0 copy-done.1
  17.4 0.0 copy-done.3
  17.4 0.3 shard_map.56.mix_ref
  17.7 0.0 collective-permute-done.2.from_even
  17.7 1.9 %collective-permute-start.7 = (bf16[3,32,1024]{2,1,0:T(8,128)(2,1)S(1)}, bf16[3,32,1024]{2,1,0:T(8,128)(2,1)S(1)}, u32[]{:S(2)}, u32[]{:S(2)}) collective-permute-start(bf16[3,32,1024]{2,1,0:T(8,128)(2,1)S(1)} %get-tuple-element.20.refs_6_), channel_id=1, source_target_pairs={{32,64},{96,128},{160,192},{224,0},{64,32},{128,96},{192,160},{0,2... | collective-permute-start | bytes 589832 | tf_op jit(solution)/shard_map/ppermute | solution.py:27
  19.6 0.0 collective-permute-start.6
  19.6 7.0 %collective-permute-done.5.refs_5_ = bf16[11,32,1024]{2,1,0:T(8,128)(2,1)S(1)} collective-permute-done((bf16[11,32,1024]{2,1,0:T(8,128)(2,1)S(1)}, bf16[11,32,1024]{2,1,0:T(8,128)(2,1)S(1)}, u32[]{:S(2)}, u32[]{:S(2)}) %collective-permute-start.5) | collective-permute-done | bytes 720928 | tf_op jit(solution)/shard_map/ppermute | solution.py:27
  26.5 0.0 collective-permute-done.4.refs_4_
  26.5 0.0 copy-done
  26.5 0.0 copy-done.2
  26.5 3.7 %shard_map.58 = (f32[32,8,1024]{2,1,0:T(8,128)S(1)}, f32[6,32,1024]{2,1,0:T(8,128)S(1)}) custom-call(bf16[256,256]{1,0:T(8,128)(2,1)S(1)} %shard_map.56.mix_ref, f32[8,16,1024]{2,1,0:T(8,128)S(1)} %copy-done, f32[8,16,1024]{2,1,0:T(8,128)S(1)} %copy-done.2, bf16[72,1024]{1,0:T(8,128)(2,1)S(1)} %get-tuple-element.14.own.refs_0_, ...), custom_call_target="tpu_custom_call" | custom-call | flops 2952790016 | bytes 4194304 | tf_op jit(solution)/shard_map/pallas_call | solution.py:253
  30.3 3.9 %collective-permute-done.3.from_odd = bf16[112,1024]{1,0:T(8,128)(2,1)S(1)} collective-permute-done((bf16[112,1024]{1,0:T(8,128)(2,1)S(1)}, bf16[112,1024]{1,0:T(8,128)(2,1)S(1)}, u32[]{:S(2)}, u32[]{:S(2)}) %collective-permute-start.3) | collective-permute-done | bytes 229408 | tf_op jit(solution)/shard_map/ppermute | solution.py:27
  34.1 0.0 collective-permute-done.7.refs_8_
  34.1 0.0 collective-permute-done.6.refs_7_
  34.1 2.5 %shard_map.59 = f32[32,16,1024]{2,1,0:T(8,128)} custom-call(bf16[256,256]{1,0:T(8,128)(2,1)S(1)} %shard_map.56.mix_ref, f32[8,16,1024]{2,1,0:T(8,128)S(1)} %copy-done, f32[8,16,1024]{2,1,0:T(8,128)S(1)} %copy-done.2, bf16[112,1024]{1,0:T(8,128)(2,1)S(1)} %collective-permute-done.2.from_even, bf16[112,1024]{1,0:T(8,128)(2,1)S(1)} %collective-permute-done.3.from_odd, ...), custom_call_target="tpu_custom_call" | custom-call | flops 1342177280 | bytes 4194304 | tf_op jit(solution)/shard_map/pallas_call | solution.py:335
  (1 shorter events, 0.0 us)
Async XLA Ops:
  1.6 6.9 %collective-permute-start.1 = (bf16[72,1024]{1,0:T(8,128)(2,1)S(1)}, bf16[72,1024]{1,0:T(8,128)(2,1)S(1)}, u32[]{:S(2)}, u32[]{:S(2)}) collective-permute-start(bf16[72,1024]{1,0:T(8,128)(2,1)S(1)} %get-tuple-element.14.own.refs_0_), channel_id=1, source_target_pairs={{32,64},{96,128},{160,192},{224,0},{64,32},{128,96},{192,160},{0,2... | collective-permute-start | bytes 442376 | tf_op jit(solution)/shard_map/ppermute | solution.py:27
  3.7 4.8 %collective-permute-start = (bf16[72,1024]{1,0:T(8,128)(2,1)S(1)}, bf16[72,1024]{1,0:T(8,128)(2,1)S(1)}, u32[]{:S(2)}, u32[]{:S(2)}) collective-permute-start(bf16[72,1024]{1,0:T(8,128)(2,1)S(1)} %get-tuple-element.14.own.refs_0_), channel_id=1, source_target_pairs={{0,32},{64,96},{128,160},{192,224},{32,0},{96,64},{160,128},{224,1... | collective-permute-start | bytes 442376 | tf_op jit(solution)/shard_map/ppermute | solution.py:27
  4.1 22.4 %collective-permute-start.5 = (bf16[11,32,1024]{2,1,0:T(8,128)(2,1)S(1)}, bf16[11,32,1024]{2,1,0:T(8,128)(2,1)S(1)}, u32[]{:S(2)}, u32[]{:S(2)}) collective-permute-start(bf16[11,32,1024]{2,1,0:T(8,128)(2,1)S(1)} %get-tuple-element.18.refs_3_), channel_id=1, source_target_pairs={{32,64},{96,128},{160,192},{224,0},{64,32},{128,96},{192,160},{0,2... | collective-permute-start | bytes 2162696 | tf_op jit(solution)/shard_map/ppermute | solution.py:27
  5.2 21.3 %collective-permute-start.4 = (bf16[11,32,1024]{2,1,0:T(8,128)(2,1)S(1)}, bf16[11,32,1024]{2,1,0:T(8,128)(2,1)S(1)}, u32[]{:S(2)}, u32[]{:S(2)}) collective-permute-start(bf16[11,32,1024]{2,1,0:T(8,128)(2,1)S(1)} %get-tuple-element.18.refs_3_), channel_id=1, source_target_pairs={{0,32},{64,96},{128,160},{192,224},{32,0},{96,64},{160,128},{224,1... | collective-permute-start | bytes 2162696 | tf_op jit(solution)/shard_map/ppermute | solution.py:27
  8.5 8.9 %copy-start.1 = (s32[2,8,32,32]{3,2,1,0:T(8,128)S(1)}, s32[2,8,32,32]{3,2,1,0:T(8,128)}, u32[]{:S(2)}) copy-start(s32[2,8,32,32]{3,2,1,0:T(8,128)} %pattern_ref.1) | copy-start | bytes 196612
  8.5 8.9 %copy-start.3 = (bf16[2,8,32,32]{3,2,1,0:T(8,128)(2,1)S(1)}, bf16[2,8,32,32]{3,2,1,0:T(8,128)(2,1)}, u32[]{:S(2)}) copy-start(bf16[2,8,32,32]{3,2,1,0:T(8,128)(2,1)} %coupling_ref.1) | copy-start | bytes 98308
  8.5 18.0 %copy-start = (f32[8,16,1024]{2,1,0:T(8,128)S(1)}, f32[8,16,1024]{2,1,0:T(8,128)}, u32[]{:S(2)}) copy-start(f32[8,16,1024]{2,1,0:T(8,128)} %kx_ref.3) | copy-start | bytes 1572868
  8.5 18.0 %copy-start.2 = (f32[8,16,1024]{2,1,0:T(8,128)S(1)}, f32[8,16,1024]{2,1,0:T(8,128)}, u32[]{:S(2)}) copy-start(f32[8,16,1024]{2,1,0:T(8,128)} %ky_ref.3) | copy-start | bytes 1572868
  8.6 9.1 %collective-permute-start.2 = (bf16[112,1024]{1,0:T(8,128)(2,1)S(1)}, bf16[112,1024]{1,0:T(8,128)(2,1)S(1)}, u32[]{:S(2)}, u32[]{:S(2)}) collective-permute-start(bf16[112,1024]{1,0:T(8,128)(2,1)S(1)} %get-tuple-element.16), channel_id=1, source_target_pairs={{0,1},{2,3},{4,5},{6,7},{8,9},{10,11},{12,13},{14,15},{16,17},{18,... | collective-permute-start | bytes 688136 | tf_op jit(solution)/shard_map/ppermute | solution.py:27
  11.6 22.6 %collective-permute-start.3 = (bf16[112,1024]{1,0:T(8,128)(2,1)S(1)}, bf16[112,1024]{1,0:T(8,128)(2,1)S(1)}, u32[]{:S(2)}, u32[]{:S(2)}) collective-permute-start(bf16[112,1024]{1,0:T(8,128)(2,1)S(1)} %get-tuple-element.17), channel_id=1, source_target_pairs={{1,2},{3,4},{5,6},{7,8},{9,10},{11,12},{13,14},{15,16},{17,18},{19... | collective-permute-start | bytes 688136 | tf_op jit(solution)/shard_map/ppermute | solution.py:27
  17.7 16.4 %collective-permute-start.7 = (bf16[3,32,1024]{2,1,0:T(8,128)(2,1)S(1)}, bf16[3,32,1024]{2,1,0:T(8,128)(2,1)S(1)}, u32[]{:S(2)}, u32[]{:S(2)}) collective-permute-start(bf16[3,32,1024]{2,1,0:T(8,128)(2,1)S(1)} %get-tuple-element.20.refs_6_), channel_id=1, source_target_pairs={{32,64},{96,128},{160,192},{224,0},{64,32},{128,96},{192,160},{0,2... | collective-permute-start | bytes 589832 | tf_op jit(solution)/shard_map/ppermute | solution.py:27
  19.6 14.6 %collective-permute-start.6 = (bf16[3,32,1024]{2,1,0:T(8,128)(2,1)S(1)}, bf16[3,32,1024]{2,1,0:T(8,128)(2,1)S(1)}, u32[]{:S(2)}, u32[]{:S(2)}) collective-permute-start(bf16[3,32,1024]{2,1,0:T(8,128)(2,1)S(1)} %get-tuple-element.20.refs_6_), channel_id=1, source_target_pairs={{0,32},{64,96},{128,160},{192,224},{32,0},{96,64},{160,128},{224,1... | collective-permute-start | bytes 589832 | tf_op jit(solution)/shard_map/ppermute | solution.py:27

commit v4 on v3

--- a/solution.py
+++ b/solution.py
@@ -11,6 +11,7 @@
 PIECE = 256
 EIGHT = 8
 KTERMS = 8
+RUN = 8
 EARLY = 11
 FORWARD_COST = 1 << 34
 BF16 = jnp.bfloat16
@@ -20,11 +21,21 @@
 OFF_CHIP = pl.BlockSpec(memory_space=pltpu.HBM)
 
 
-def swapped(x, axis, first, wraps):
-    count = lax.axis_size(axis)
-    starts = [i for i in range(first, count, 2) if wraps or i + 1 < count]
-    pairs = [(i, (i + 1) % count) for i in starts]
-    return lax.ppermute(x, axis, pairs + [(j, i) for i, j in pairs])
+def swapped(x, first):
+    count = lax.axis_size("mode")
+    pairs = [(i, (i + 1) % count) for i in range(first, count, 2)]
+    return lax.ppermute(x, "mode", pairs + [(j, i) for i, j in pairs])
+
+
+def swapped_inside(x, first):
+    count = lax.axis_size("space")
+    pairs = [(i, i + 1) for i in range(first, count - 1, 2) if (i + 1) % RUN]
+    return lax.ppermute(x, "space", pairs + [(j, i) for i, j in pairs])
+
+
+def swapped_between(x):
+    pairs = [(i - 1, i) for i in range(RUN, lax.axis_size("space"), RUN)]
+    return lax.ppermute(x, "space", pairs + [(j, i) for i, j in pairs])
 
 
 def odd_index(axis):
@@ -66,14 +77,8 @@
         pltpu.make_async_copy(pattern_hbm.at[1], pattern_ref, sems.at[count + 1]),
         pltpu.make_async_copy(kx_hbm.at[:, rows - EIGHT :, :], kx_ref, sems.at[count + 2]),
     ]
-    for copy in small[:2] + copies + small[2:]:
+    for copy in copies + small:
         copy.start()
-    for copy in small[:2]:
-        copy.wait()
-    coef = jnp.where(pattern_ref[...] > 0, coupling_ref[...].astype(F32), 0.0)
-    flat = jnp.concatenate([coef[k] for k in range(coef.shape[0])], axis=1)
-    packed = [flat[n * EIGHT : (n + 1) * EIGHT] for n in range(modes // EIGHT)]
-    rim[2 * modes :] = jnp.concatenate(packed, axis=1).astype(BF16)
     for n, copy in enumerate(copies):
         at = slice(n * wide, (n + 1) * wide)
         copy.wait()
@@ -82,6 +87,12 @@
         rim[modes : 2 * modes, at] = turned[rows - 1]
         early[:, :, at] = turned[1 : 1 + EARLY]
         late[:, :, at] = turned[1 + EARLY : rows - 1]
+    for copy in small[:2]:
+        copy.wait()
+    coef = jnp.where(pattern_ref[...] > 0, coupling_ref[...].astype(F32), 0.0)
+    flat = jnp.concatenate([coef[k] for k in range(coef.shape[0])], axis=1)
+    packed = [flat[n * EIGHT : (n + 1) * EIGHT] for n in range(modes // EIGHT)]
+    rim[2 * modes :] = jnp.concatenate(packed, axis=1).astype(BF16)
     small[2].wait()
     kappa = kx_ref[:, EIGHT - 1, :]
     whole = kappa.astype(BF16)
@@ -269,39 +280,116 @@
     )(mix, kappa_x, kappa_y, *rims, *inner)
 
 
-def late_body(mix_ref, kx_ref, ky_ref, from_even, from_odd, *refs):
-    (own, even, odd), inner, last = refs[:3], refs[3:6], refs[6:9]
-    front, spare, image, stack, ahead, edge_kx, laid, out, sems = refs[9:]
+def run_end_body(mix_ref, own, even, odd, edge, ends, row):
+    modes = ends.shape[0] // 3
+    cols = ends.shape[1]
+    last = lax.rem(lax.axis_index("space"), RUN) == RUN - 1
+
+    @pl.when(jnp.logical_not(last))
+    def _():
+        for n, block in enumerate((own, even, odd)):
+            ends[n * modes : (n + 1) * modes] = block[:modes]
+
+    @pl.when(last)
+    def _():
+        pile(row, 0, *(x[modes : 2 * modes] for x in (own, even, odd)))
+        kappa = edge[:KTERMS].astype(F32) + edge[KTERMS:].astype(F32)
+        for c in range(0, cols, TILE):
+            at = slice(c, c + TILE)
+            w = jnp.dot(mix_ref[:, 4 * modes :], row[0, :, at], preferred_element_type=F32)
+            total = weighted(w, lambda k: kappa[k : k + 1, at])
+            whole = total.astype(BF16)
+            ends[:modes, at] = whole
+            ends[modes : 2 * modes, at] = (total - whole.astype(F32)).astype(BF16)
+        ends[2 * modes :] = jnp.concatenate([edge[...]] * (modes // edge.shape[0]), axis=0)
+
+
+def run_end(modes, mix, rims, edge):
+    cols = edge.shape[1]
+    return pl.pallas_call(
+        run_end_body,
+        out_shape=jax.ShapeDtypeStruct((3 * modes, cols), BF16),
+        in_specs=[ON_CHIP] * 5,
+        out_specs=ON_CHIP,
+        scratch_shapes=[pltpu.VMEM((1, 4 * modes, cols), BF16)],
+        compiler_params=room(4),
+        cost_estimate=cost(2 * KTERMS * modes * 4 * modes * cols, 1 << 20),
+    )(mix, *rims, edge)
+
+
+def edges_body(
+    mix_ref, kx_ref, from_even, from_odd, between, own, even, odd, front, whole, face, stack, edge_kx
+):
+    modes, _, cols = front.shape
+    rows = kx_ref.shape[1]
+    flip = odd_index("space")
+    turn = lax.rem(lax.axis_index("space"), RUN)
+
+    def either(flipped, at):
+        first, second = (from_even, from_odd) if flipped else (from_odd, from_even)
+        return jnp.where(flip, first[at].astype(F32), second[at].astype(F32))
+
+    def blocks(flipped):
+        for n in range(3):
+            at = slice(n * modes, (n + 1) * modes)
+            value = either(flipped, at)
+            if not flipped:
+                value = jnp.where(turn == RUN - 1, between[at].astype(F32), value)
+            yield value.astype(BF16)
+
+    pieces = jnp.where(
+        turn == 0,
+        between[2 * modes : 2 * modes + 2 * KTERMS].astype(F32),
+        either(True, slice(3 * modes, None)),
+    )
+    edge_kx[...] = pieces[:KTERMS] + pieces[KTERMS:]
+    pile(stack, 0, *blocks(True))
+    pile(stack, 1, *(x[:modes] for x in (own, even, odd)))
+    pile(stack, 2, *(x[modes : 2 * modes] for x in (own, even, odd)))
+    pile(stack, 3, *blocks(False))
+    for c in range(0, cols, TILE):
+        at = slice(c, c + TILE)
+        other = between[:modes, at].astype(F32) + between[modes : 2 * modes, at].astype(F32)
+        above = row_flux(mix_ref, stack, 0, at, lambda k: edge_kx[k : k + 1, at])
+        whole[:, 0, at] = front[:, 0, at] + (above - jnp.where(turn == 0, other, 0.0))
+        face[:, at] = row_flux(mix_ref, stack, 2, at, lambda k: kx_ref[k, rows - 1 : rows, at])
+
+
+def edge_faces(mix, kappa_x, from_even, from_odd, between, rims, front):
+    modes, _, cols = front.shape
+    return pl.pallas_call(
+        edges_body,
+        out_shape=(jax.ShapeDtypeStruct(front.shape, F32), jax.ShapeDtypeStruct((modes, cols), F32)),
+        in_specs=[ON_CHIP] * 9,
+        out_specs=(ON_CHIP, ON_CHIP),
+        scratch_shapes=[
+            pltpu.VMEM((4, 4 * modes, cols), BF16),
+            pltpu.VMEM((KTERMS, cols), F32),
+        ],
+        input_output_aliases={8: 0},
+        compiler_params=room(12),
+        cost_estimate=cost(4 * KTERMS * modes * 8 * modes * cols, 1 << 20),
+    )(mix, kappa_x, from_even, from_odd, between, *rims, front)
+
+
+def late_body(mix_ref, kx_ref, ky_ref, *refs):
+    rims, inner, last, (front, spare, face), (image, stack, ahead, laid, out, sems) = (
+        refs[:3],
+        refs[3:6],
+        refs[6:9],
+        refs[9:12],
+        refs[12:],
+    )
     modes = front.shape[0]
     rows, cols = kx_ref.shape[1:]
     count = rows - EARLY
-    flip = odd_index("space")
-
-    def either(flipped, at):
-        first, second = (from_even, from_odd) if flipped else (from_odd, from_even)
-        return jnp.where(flip, first[at].astype(F32), second[at].astype(F32))
-
-    def blocks(flipped):
-        return (either(flipped, slice(n * modes, (n + 1) * modes)).astype(BF16) for n in range(3))
-
-    kappa = either(True, slice(3 * modes, None))
-    edge_kx[...] = kappa[:KTERMS] + kappa[KTERMS:]
-    pile(stack, 0, *blocks(True))
-    pile(stack, 1, own[:modes], even[:modes], odd[:modes])
-    for c in range(0, cols, TILE):
-        at = slice(c, c + TILE)
-        above = row_flux(mix_ref, stack, 0, at, lambda k: edge_kx[k : k + 1, at])
-        out[0, :, :, at] = front[:, :, at]
-        out[0, :, 0, at] = front[:, 0, at] + above
-    sends = [pltpu.make_async_copy(out.at[0], image.at[:, :EIGHT, :], sems.at[0])]
+    sends = [pltpu.make_async_copy(front, image.at[:, :EIGHT, :], sems.at[0])]
     sends[0].start()
-
-    pile(stack, 2, *(x[EARLY - 1] for x in inner))
+    pile(stack, 0, *(x[EARLY - 1] for x in inner))
     for n in range(count - 2):
-        pile(stack, 3 + n, *(x[n] for x in last))
-    pile(stack, count + 1, *(x[modes : 2 * modes] for x in (own, even, odd)))
-    pile(stack, count + 2, *blocks(False))
-    look_ahead(stack, ahead, 3, count - 2)
+        pile(stack, 1 + n, *(x[n] for x in last))
+    pile(stack, count - 1, *(x[modes : 2 * modes] for x in rims))
+    look_ahead(stack, ahead, 1, count - 2)
     carry = [jnp.zeros((modes, 1), F32)] * (count - 2)
     for c in range(0, cols, TILE):
         at = slice(c, c + TILE)
@@ -310,63 +398,67 @@
         behind = spare[EARLY - EIGHT, :, at]
         for m in range(count):
             i = EARLY + m
-            here = row_flux(mix_ref, stack, 2 + m, at, lambda k: kx_ref[k, i : i + 1, at])
+            if m < count - 1:
+                here = row_flux(mix_ref, stack, m, at, lambda k: kx_ref[k, i : i + 1, at])
+            else:
+                here = face[:, at]
             if 0 < m < count - 1:
-                right = column_flux(mix_ref, stack, ahead, 2 + m, m - 1, at, lambda k: ky_ref[k, i : i + 1, at])
+                right = column_flux(mix_ref, stack, ahead, m, m - 1, at, lambda k: ky_ref[k, i : i + 1, at])
                 left, carry[m - 1] = shifted(right, carry[m - 1])
                 across = left - right
             else:
                 across = spare[EARLY - EIGHT + 1 + (m > 0), :, at]
             laid[i - EIGHT, :, at] = (behind - here) + across
             behind = here
-        out[1, :, :, at] = jnp.swapaxes(laid[:, :, at], 0, 1)
+        out[:, :, at] = jnp.swapaxes(laid[:, :, at], 0, 1)
         sends.append(
-            pltpu.make_async_copy(out.at[1, :, :, at], image.at[:, EIGHT:, at], sems.at[1 + c // TILE])
+            pltpu.make_async_copy(out.at[:, :, at], image.at[:, EIGHT:, at], sems.at[1 + c // TILE])
         )
         sends[-1].start()
     for send in sends:
         send.wait()
 
 
-def late_image(mix, kappa_x, kappa_y, from_even, from_odd, rims, inner, last, front, spare):
+def late_image(mix, kappa_x, kappa_y, rims, inner, last, front, spare, face):
     kterms, rows, cols = kappa_x.shape
     modes = inner[0].shape[1]
     count = rows - EARLY
     return pl.pallas_call(
         late_body,
         out_shape=jax.ShapeDtypeStruct((modes, rows, cols), F32),
-        in_specs=[ON_CHIP] * 16,
+        in_specs=[ON_CHIP] * 15,
         out_specs=OFF_CHIP,
         scratch_shapes=[
-            pltpu.VMEM((count + 3, 4 * modes, cols), BF16),
+            pltpu.VMEM((count, 4 * modes, cols), BF16),
             pltpu.VMEM((count - 2, 3 * modes, cols), BF16),
-            pltpu.VMEM((kterms, cols), F32),
             pltpu.VMEM((EIGHT, modes, cols), F32),
-            pltpu.VMEM((2, modes, EIGHT, cols), F32),
+            pltpu.VMEM((modes, EIGHT, cols), F32),
             pltpu.SemaphoreType.DMA((1 + cols // TILE,)),
         ],
         compiler_params=room(20),
         cost_estimate=cost(4 * count * kterms * modes * 8 * modes * cols, 4 << 20),
-    )(mix, kappa_x, kappa_y, from_even, from_odd, *rims, *inner, *last, front, spare)
+    )(mix, kappa_x, kappa_y, *rims, *inner, *last, front, spare, face)
 
 
 def shards(field, kappa_x, kappa_y, coupling, pattern):
     rim, inner, last, edge = split_rows(field, coupling, pattern, kappa_x)
 
     def over_mode(x):
-        return x, swapped(x, "mode", 0, True), swapped(x, "mode", 1, True)
+        return x, swapped(x, 0), swapped(x, 1)
 
     rims = over_mode(rim)
     inners = over_mode(inner)
     to_even, to_odd = forward_rows(field.shape[0], *rims, edge)
-    from_even = swapped(to_even, "space", 0, False)
-    from_odd = swapped(to_odd, "space", 1, False)
+    from_even = swapped_inside(to_even, 0)
+    from_odd = swapped_inside(to_odd, 1)
     mix = mixing(coupling, pattern, *rims[1:])
-    last = lax.optimization_barrier((last, from_even))[0]
+    last_odd = swapped(lax.optimization_barrier((last, from_even))[0], 1)
+    last_even = swapped(lax.optimization_barrier((last, from_odd))[0], 0)
+    between = swapped_between(run_end(field.shape[0], mix, rims, edge))
     front, spare = early_image(mix, kappa_x, kappa_y, rims, inners)
-    return late_image(
-        mix, kappa_x, kappa_y, from_even, from_odd, rims, inners, over_mode(last), front, spare
-    )
+    front, face = edge_faces(mix, kappa_x, from_even, from_odd, between, rims, front)
+    lasts = (last, last_even, last_odd)
+    return late_image(mix, kappa_x, kappa_y, rims, inners, lasts, front, spare, face)
 
 
 def solution(mesh):

time: 37.2 us -> 36.1 us (0.970); the launches traced: 36.6 us -> 36 us
  waiting for transfers between devices: 14.1 us -> 9.66 us
  starting transfers between devices: 14.4 us -> 17.8 us
    ppermute x8 -> x9, waiting for transfers between devices: 14.1 us -> 9.66 us  [the longest x6 5.97 us: swapped(): return lax.ppermute(x, 'mode', pairs + [(j, i) for i, j in pairs])]
    ppermute x8 -> x9, starting transfers between devices: 14.4 us -> 17.8 us  [the longest x1 7.08 us: swapped_between(): return lax.ppermute(x, 'space', pairs + [(j, i) for i, j in pairs])]
    pallas_call x0 -> x2, Pallas kernels: none -> 0.78 us  [the longest x1 0.48 us: edge_faces(): pl.pallas_call(edges_body, out_shape=(jax.ShapeDtypeStruct(front.shape, F...]
    pallas_call x1, Pallas kernels: 2.46 us -> 2.05 us  [late_image(): pl.pallas_call(late_body, out_shape=jax.ShapeDtypeStruct((modes, rows, co...]
  transfers between devices with their start and end apart: 8 -> 9, of which waited for: 3 -> 3; matrix products, arithmetic and copies ran while one was open for 0% -> 0% of each run, Pallas kernels for 11% -> 13%
where the time goes in v4:
time: 36.1 us; the launch traced here: 36 us
  starting transfers between devices  17.8 us (49%)
  waiting for transfers between devices  9.66 us (27%)
  Pallas kernels  8.39 us (23%)
    ppermute x1, starting transfers between devices, swapped_between(): return lax.ppermute(x, 'space', pairs + [(j, i) for i, j in pairs])  7.08 us
    ppermute x6, waiting for transfers between devices, swapped(): return lax.ppermute(x, 'mode', pairs + [(j, i) for i, j in pairs])  5.97 us
    ppermute x6, starting transfers between devices, swapped(): return lax.ppermute(x, 'mode', pairs + [(j, i) for i, j in pairs])  5.63 us
    ppermute x2, starting transfers between devices, swapped_inside(): return lax.ppermute(x, 'space', pairs + [(j, i) for i, j in pairs])  5.05 us
    pallas_call x1, Pallas kernels, early_image(): pl.pallas_call(early_body, out_shape=(jax.ShapeDtypeStruct((modes, EIGHT,...  3.71 us
    ppermute x1, waiting for transfers between devices, swapped_between(): return lax.ppermute(x, 'space', pairs + [(j, i) for i, j in pairs])  3.68 us
    pallas_call x1, Pallas kernels, late_image(): pl.pallas_call(late_body, out_shape=jax.ShapeDtypeStruct((modes, rows, co...  2.05 us
    pallas_call x1, Pallas kernels, split_rows(): pl.pallas_call(split_body, out_shape=(jax.ShapeDtypeStruct((2 * modes + e...  1.54 us
  transfers between devices with their start and end apart: 9, of which 3 were waited for; matrix products, arithmetic and copies ran while one was open for 0% of the time, Pallas kernels for 13%

profile of v4, /device:TPU:121, one launch (start us, length us, event | category | flops | bytes accessed | tf_op | source)
XLA Modules:
  0.0 36.0 jit_solution(11606762760595376348)
XLA Ops:
  0.0 1.5 %shard_map.55 = (bf16[72,1024]{1,0:T(8,128)(2,1)S(1)}, bf16[11,32,1024]{2,1,0:T(8,128)(2,1)S(1)}, bf16[3,32,1024]{2,1,0:T(8,128)(2,1)S(1)}, bf16[16,1024]{1,0:T(8,128)(2,1)S(1)}) custom-call(bf16[32,16,1024]{2,1,0:T(8,128)(2,1)} %field_hbm.1, bf16[2,8,32,32]{3,2,1,0:T(8,128)(2,1)} %coupling_ref.1, s32[2,8,32,32]{3,2,1,0:T(8,128)} %pattern_ref.1, ...), custom_call_target="tpu_custom_call" | custom-call | bytes 2097152 | tf_op jit(solution)/shard_map/pallas_call | solution.py:105
  1.6 2.1 %collective-permute-start.1 = (bf16[72,1024]{1,0:T(8,128)(2,1)S(1)}, bf16[72,1024]{1,0:T(8,128)(2,1)S(1)}, u32[]{:S(2)}, u32[]{:S(2)}) collective-permute-start(bf16[72,1024]{1,0:T(8,128)(2,1)S(1)} %get-tuple-element.17.own.refs_0_), channel_id=1, source_target_pairs={{32,64},{96,128},{160,192},{224,0},{64,32},{128,96},{192,160},{0,2... | collective-permute-start | bytes 442376 | tf_op jit(solution)/shard_map/ppermute | solution.py:27
  3.7 0.4 %collective-permute-start = (bf16[72,1024]{1,0:T(8,128)(2,1)S(1)}, bf16[72,1024]{1,0:T(8,128)(2,1)S(1)}, u32[]{:S(2)}, u32[]{:S(2)}) collective-permute-start(bf16[72,1024]{1,0:T(8,128)(2,1)S(1)} %get-tuple-element.17.own.refs_0_), channel_id=1, source_target_pairs={{0,32},{64,96},{128,160},{192,224},{32,0},{96,64},{160,128},{224,1... | collective-permute-start | bytes 442376 | tf_op jit(solution)/shard_map/ppermute | solution.py:27
  4.1 1.2 %collective-permute-start.3 = (bf16[11,32,1024]{2,1,0:T(8,128)(2,1)S(1)}, bf16[11,32,1024]{2,1,0:T(8,128)(2,1)S(1)}, u32[]{:S(2)}, u32[]{:S(2)}) collective-permute-start(bf16[11,32,1024]{2,1,0:T(8,128)(2,1)S(1)} %get-tuple-element.18.refs_3_), channel_id=1, source_target_pairs={{32,64},{96,128},{160,192},{224,0},{64,32},{128,96},{192,160},{0,2... | collective-permute-start | bytes 2162696 | tf_op jit(solution)/shard_map/ppermute | solution.py:27
  5.2 0.0 collective-permute-start.2
  5.2 3.2 %collective-permute-done.1.odd.refs_2_ = bf16[72,1024]{1,0:T(8,128)(2,1)S(1)} collective-permute-done((bf16[72,1024]{1,0:T(8,128)(2,1)S(1)}, bf16[72,1024]{1,0:T(8,128)(2,1)S(1)}, u32[]{:S(2)}, u32[]{:S(2)}) %collective-permute-start.1) | collective-permute-done | bytes 147488 | tf_op jit(solution)/shard_map/ppermute | solution.py:27
  8.5 0.0 collective-permute-done.even.refs_1_
  8.5 0.0 copy-start.1
  8.5 0.0 copy-start.3
  8.5 0.0 copy-start
  8.5 0.0 copy-start.2
  8.5 0.8 %collective-permute-start.4 = (bf16[112,1024]{1,0:T(8,128)(2,1)S(1)}, bf16[112,1024]{1,0:T(8,128)(2,1)S(1)}, u32[]{:S(2)}, u32[]{:S(2)}) collective-permute-start(bf16[112,1024]{1,0:T(8,128)(2,1)S(1)} %get-tuple-element.21), channel_id=1, source_target_pairs={{1,2},{3,4},{5,6},{9,10},{11,12},{13,14},{17,18},{19,20},{21,22},{... | collective-permute-start | bytes 688136 | tf_op jit(solution)/shard_map/ppermute | solution.py:33
  9.4 4.2 %collective-permute-start.6 = (bf16[112,1024]{1,0:T(8,128)(2,1)S(1)}, bf16[112,1024]{1,0:T(8,128)(2,1)S(1)}, u32[]{:S(2)}, u32[]{:S(2)}) collective-permute-start(bf16[112,1024]{1,0:T(8,128)(2,1)S(1)} %get-tuple-element.23), channel_id=1, source_target_pairs={{0,1},{2,3},{4,5},{6,7},{8,9},{10,11},{12,13},{14,15},{16,17},{18,... | collective-permute-start | bytes 688136 | tf_op jit(solution)/shard_map/ppermute | solution.py:33
  13.6 0.0 copy-done.1
  13.6 0.0 copy-done.3
  13.6 0.3 shard_map.56.mix_ref
  13.9 0.3 shard_map.58
  14.2 7.1 %collective-permute-start.8 = (bf16[96,1024]{1,0:T(8,128)(2,1)S(1)}, bf16[96,1024]{1,0:T(8,128)(2,1)S(1)}, u32[]{:S(2)}, u32[]{:S(2)}) collective-permute-start(bf16[96,1024]{1,0:T(8,128)(2,1)S(1)} %shard_map.58), channel_id=1, source_target_pairs={{7,8},{15,16},{23,24},{8,7},{16,15},{24,23},{39,40},{47,48},{55,56... | collective-permute-start | bytes 589832 | tf_op jit(solution)/shard_map/ppermute | solution.py:38
  21.3 0.0 collective-permute-done.4.from_odd
  21.3 0.1 collective-permute-start.5
  21.4 0.0 collective-permute-done.6.from_even
  21.4 1.9 %collective-permute-start.7 = (bf16[3,32,1024]{2,1,0:T(8,128)(2,1)S(1)}, bf16[3,32,1024]{2,1,0:T(8,128)(2,1)S(1)}, u32[]{:S(2)}, u32[]{:S(2)}) collective-permute-start(bf16[3,32,1024]{2,1,0:T(8,128)(2,1)S(1)} %get-tuple-element.24.refs_6_), channel_id=1, source_target_pairs={{32,64},{96,128},{160,192},{224,0},{64,32},{128,96},{192,160},{0,2... | collective-permute-start | bytes 589832 | tf_op jit(solution)/shard_map/ppermute | solution.py:27
  23.3 2.7 %collective-permute-done.3.refs_5_ = bf16[11,32,1024]{2,1,0:T(8,128)(2,1)S(1)} collective-permute-done((bf16[11,32,1024]{2,1,0:T(8,128)(2,1)S(1)}, bf16[11,32,1024]{2,1,0:T(8,128)(2,1)S(1)}, u32[]{:S(2)}, u32[]{:S(2)}) %collective-permute-start.3) | collective-permute-done | bytes 720928 | tf_op jit(solution)/shard_map/ppermute | solution.py:27
  26.0 0.0 collective-permute-done.2.refs_4_
  26.0 0.0 copy-done
  26.0 0.0 copy-done.2
  26.0 3.7 %shard_map.59 = (f32[32,8,1024]{2,1,0:T(8,128)S(1)}, f32[6,32,1024]{2,1,0:T(8,128)S(1)}) custom-call(bf16[256,256]{1,0:T(8,128)(2,1)S(1)} %shard_map.56.mix_ref, f32[8,16,1024]{2,1,0:T(8,128)S(1)} %copy-done, f32[8,16,1024]{2,1,0:T(8,128)S(1)} %copy-done.2, bf16[72,1024]{1,0:T(8,128)(2,1)S(1)} %get-tuple-element.17.own.refs_0_, ...), custom_call_target="tpu_custom_call" | custom-call | flops 2952790016 | bytes 4194304 | tf_op jit(solution)/shard_map/pallas_call | solution.py:264
  29.7 3.7 %collective-permute-done.8.between = bf16[96,1024]{1,0:T(8,128)(2,1)S(1)} collective-permute-done((bf16[96,1024]{1,0:T(8,128)(2,1)S(1)}, bf16[96,1024]{1,0:T(8,128)(2,1)S(1)}, u32[]{:S(2)}, u32[]{:S(2)}) %collective-permute-start.8) | collective-permute-done | bytes 196640 | tf_op jit(solution)/shard_map/ppermute | solution.py:38
  33.4 0.5 %shard_map.60 = (f32[32,8,1024]{2,1,0:T(8,128)S(1)}, f32[32,1024]{1,0:T(8,128)S(1)}) custom-call(bf16[256,256]{1,0:T(8,128)(2,1)S(1)} %shard_map.56.mix_ref, f32[8,16,1024]{2,1,0:T(8,128)S(1)} %copy-done, bf16[112,1024]{1,0:T(8,128)(2,1)S(1)} %collective-permute-done.6.from_even, ...), custom_call_target="tpu_custom_call", output_to_operand_aliasing={{0}: (8, {})} | custom-call | flops 268435456 | bytes 1048576 | tf_op jit(solution)/shard_map/pallas_call | solution.py:360
  33.9 0.0 collective-permute-done.5.refs_7_
  33.9 0.0 collective-permute-done.7.refs_8_
  33.9 2.0 %shard_map.61 = f32[32,16,1024]{2,1,0:T(8,128)} custom-call(bf16[256,256]{1,0:T(8,128)(2,1)S(1)} %shard_map.56.mix_ref, f32[8,16,1024]{2,1,0:T(8,128)S(1)} %copy-done, f32[8,16,1024]{2,1,0:T(8,128)S(1)} %copy-done.2, bf16[72,1024]{1,0:T(8,128)(2,1)S(1)} %get-tuple-element.17.own.refs_0_, bf16[72,1024]{1,0:T(8,128)(2,1)S(1)} %collective-permute-done.even.refs_1_, ...), custom_call_target="tpu_custom_call" | custom-call | flops 1342177280 | bytes 4194304 | tf_op jit(solution)/shard_map/pallas_call | solution.py:426
  (1 shorter events, 0.0 us)
Async XLA Ops:
  1.6 6.9 %collective-permute-start.1 = (bf16[72,1024]{1,0:T(8,128)(2,1)S(1)}, bf16[72,1024]{1,0:T(8,128)(2,1)S(1)}, u32[]{:S(2)}, u32[]{:S(2)}) collective-permute-start(bf16[72,1024]{1,0:T(8,128)(2,1)S(1)} %get-tuple-element.17.own.refs_0_), channel_id=1, source_target_pairs={{32,64},{96,128},{160,192},{224,0},{64,32},{128,96},{192,160},{0,2... | collective-permute-start | bytes 442376 | tf_op jit(solution)/shard_map/ppermute | solution.py:27
  3.7 4.8 %collective-permute-start = (bf16[72,1024]{1,0:T(8,128)(2,1)S(1)}, bf16[72,1024]{1,0:T(8,128)(2,1)S(1)}, u32[]{:S(2)}, u32[]{:S(2)}) collective-permute-start(bf16[72,1024]{1,0:T(8,128)(2,1)S(1)} %get-tuple-element.17.own.refs_0_), channel_id=1, source_target_pairs={{0,32},{64,96},{128,160},{192,224},{32,0},{96,64},{160,128},{224,1... | collective-permute-start | bytes 442376 | tf_op jit(solution)/shard_map/ppermute | solution.py:27
  4.1 21.9 %collective-permute-start.3 = (bf16[11,32,1024]{2,1,0:T(8,128)(2,1)S(1)}, bf16[11,32,1024]{2,1,0:T(8,128)(2,1)S(1)}, u32[]{:S(2)}, u32[]{:S(2)}) collective-permute-start(bf16[11,32,1024]{2,1,0:T(8,128)(2,1)S(1)} %get-tuple-element.18.refs_3_), channel_id=1, source_target_pairs={{32,64},{96,128},{160,192},{224,0},{64,32},{128,96},{192,160},{0,2... | collective-permute-start | bytes 2162696 | tf_op jit(solution)/shard_map/ppermute | solution.py:27
  5.2 20.8 %collective-permute-start.2 = (bf16[11,32,1024]{2,1,0:T(8,128)(2,1)S(1)}, bf16[11,32,1024]{2,1,0:T(8,128)(2,1)S(1)}, u32[]{:S(2)}, u32[]{:S(2)}) collective-permute-start(bf16[11,32,1024]{2,1,0:T(8,128)(2,1)S(1)} %get-tuple-element.18.refs_3_), channel_id=1, source_target_pairs={{0,32},{64,96},{128,160},{192,224},{32,0},{96,64},{160,128},{224,1... | collective-permute-start | bytes 2162696 | tf_op jit(solution)/shard_map/ppermute | solution.py:27
  8.5 5.1 %copy-start.1 = (s32[2,8,32,32]{3,2,1,0:T(8,128)S(1)}, s32[2,8,32,32]{3,2,1,0:T(8,128)}, u32[]{:S(2)}) copy-start(s32[2,8,32,32]{3,2,1,0:T(8,128)} %pattern_ref.1) | copy-start | bytes 196612
  8.5 5.1 %copy-start.3 = (bf16[2,8,32,32]{3,2,1,0:T(8,128)(2,1)S(1)}, bf16[2,8,32,32]{3,2,1,0:T(8,128)(2,1)}, u32[]{:S(2)}) copy-start(bf16[2,8,32,32]{3,2,1,0:T(8,128)(2,1)} %coupling_ref.1) | copy-start | bytes 98308
  8.5 17.5 %copy-start = (f32[8,16,1024]{2,1,0:T(8,128)S(1)}, f32[8,16,1024]{2,1,0:T(8,128)}, u32[]{:S(2)}) copy-start(f32[8,16,1024]{2,1,0:T(8,128)} %kx_ref.5) | copy-start | bytes 1572868
  8.5 17.5 %copy-start.2 = (f32[8,16,1024]{2,1,0:T(8,128)S(1)}, f32[8,16,1024]{2,1,0:T(8,128)}, u32[]{:S(2)}) copy-start(f32[8,16,1024]{2,1,0:T(8,128)} %ky_ref.3) | copy-start | bytes 1572868
  8.5 12.7 %collective-permute-start.4 = (bf16[112,1024]{1,0:T(8,128)(2,1)S(1)}, bf16[112,1024]{1,0:T(8,128)(2,1)S(1)}, u32[]{:S(2)}, u32[]{:S(2)}) collective-permute-start(bf16[112,1024]{1,0:T(8,128)(2,1)S(1)} %get-tuple-element.21), channel_id=1, source_target_pairs={{1,2},{3,4},{5,6},{9,10},{11,12},{13,14},{17,18},{19,20},{21,22},{... | collective-permute-start | bytes 688136 | tf_op jit(solution)/shard_map/ppermute | solution.py:33
  9.4 12.0 %collective-permute-start.6 = (bf16[112,1024]{1,0:T(8,128)(2,1)S(1)}, bf16[112,1024]{1,0:T(8,128)(2,1)S(1)}, u32[]{:S(2)}, u32[]{:S(2)}) collective-permute-start(bf16[112,1024]{1,0:T(8,128)(2,1)S(1)} %get-tuple-element.23), channel_id=1, source_target_pairs={{0,1},{2,3},{4,5},{6,7},{8,9},{10,11},{12,13},{14,15},{16,17},{18,... | collective-permute-start | bytes 688136 | tf_op jit(solution)/shard_map/ppermute | solution.py:33
  14.2 19.2 %collective-permute-start.8 = (bf16[96,1024]{1,0:T(8,128)(2,1)S(1)}, bf16[96,1024]{1,0:T(8,128)(2,1)S(1)}, u32[]{:S(2)}, u32[]{:S(2)}) collective-permute-start(bf16[96,1024]{1,0:T(8,128)(2,1)S(1)} %shard_map.58), channel_id=1, source_target_pairs={{7,8},{15,16},{23,24},{8,7},{16,15},{24,23},{39,40},{47,48},{55,56... | collective-permute-start | bytes 589832 | tf_op jit(solution)/shard_map/ppermute | solution.py:38
  21.3 12.6 %collective-permute-start.5 = (bf16[3,32,1024]{2,1,0:T(8,128)(2,1)S(1)}, bf16[3,32,1024]{2,1,0:T(8,128)(2,1)S(1)}, u32[]{:S(2)}, u32[]{:S(2)}) collective-permute-start(bf16[3,32,1024]{2,1,0:T(8,128)(2,1)S(1)} %get-tuple-element.24.refs_6_), channel_id=1, source_target_pairs={{0,32},{64,96},{128,160},{192,224},{32,0},{96,64},{160,128},{224,1... | collective-permute-start | bytes 589832 | tf_op jit(solution)/shard_map/ppermute | solution.py:27
  21.4 12.5 %collective-permute-start.7 = (bf16[3,32,1024]{2,1,0:T(8,128)(2,1)S(1)}, bf16[3,32,1024]{2,1,0:T(8,128)(2,1)S(1)}, u32[]{:S(2)}, u32[]{:S(2)}) collective-permute-start(bf16[3,32,1024]{2,1,0:T(8,128)(2,1)S(1)} %get-tuple-element.24.refs_6_), channel_id=1, source_target_pairs={{32,64},{96,128},{160,192},{224,0},{64,32},{128,96},{192,160},{0,2... | collective-permute-start | bytes 589832 | tf_op jit(solution)/shard_map/ppermute | solution.py:27

commit v5 on v4

--- a/solution.py
+++ b/solution.py
@@ -85,14 +85,15 @@
         turned = jnp.swapaxes(pieces[n], 0, 1)
         rim[:modes, at] = turned[0]
         rim[modes : 2 * modes, at] = turned[rows - 1]
-        early[:, :, at] = turned[1 : 1 + EARLY]
+        rim[2 * modes : 3 * modes, at] = turned[1]
+        early[:, :, at] = turned[2 : 1 + EARLY]
         late[:, :, at] = turned[1 + EARLY : rows - 1]
     for copy in small[:2]:
         copy.wait()
     coef = jnp.where(pattern_ref[...] > 0, coupling_ref[...].astype(F32), 0.0)
     flat = jnp.concatenate([coef[k] for k in range(coef.shape[0])], axis=1)
     packed = [flat[n * EIGHT : (n + 1) * EIGHT] for n in range(modes // EIGHT)]
-    rim[2 * modes :] = jnp.concatenate(packed, axis=1).astype(BF16)
+    rim[3 * modes :] = jnp.concatenate(packed, axis=1).astype(BF16)
     small[2].wait()
     kappa = kx_ref[:, EIGHT - 1, :]
     whole = kappa.astype(BF16)
@@ -105,8 +106,8 @@
     return pl.pallas_call(
         split_body,
         out_shape=(
-            jax.ShapeDtypeStruct((2 * modes + extra, cols), BF16),
-            jax.ShapeDtypeStruct((EARLY, modes, cols), BF16),
+            jax.ShapeDtypeStruct((3 * modes + extra, cols), BF16),
+            jax.ShapeDtypeStruct((EARLY - 1, modes, cols), BF16),
             jax.ShapeDtypeStruct((rows - 2 - EARLY, modes, cols), BF16),
             jax.ShapeDtypeStruct((2 * kappa_x.shape[0], cols), BF16),
         ),
@@ -162,7 +163,7 @@
     coef = jnp.where(pattern_ref[...] > 0, coupling_ref[...].astype(F32), 0.0)
     half = coef[0] * 0.5
     flip = odd_index("mode")
-    packed = jnp.where(flip, even[2 * modes :].astype(F32), odd[2 * modes :].astype(F32))
+    packed = jnp.where(flip, even[3 * modes :].astype(F32), odd[3 * modes :].astype(F32))
     wide = packed.shape[1] * EIGHT // modes
     low = jnp.concatenate([packed[:, n * wide : (n + 1) * wide] for n in range(modes // EIGHT)], axis=0).T
     own, turned, up = (
@@ -231,8 +232,9 @@
     modes = front.shape[0]
     cols = front.shape[2]
     pile(stack, 0, own[:modes], even[:modes], odd[:modes])
-    for n in range(EARLY):
-        pile(stack, 1 + n, *(x[n] for x in inner))
+    pile(stack, 1, *(x[2 * modes : 3 * modes] for x in (own, even, odd)))
+    for n in range(EARLY - 1):
+        pile(stack, 2 + n, *(x[n] for x in inner))
     pile(stack, EARLY + 1, *(x[modes : 2 * modes] for x in (own, even, odd)))
     look_ahead(stack, ahead, 0, EARLY + 2)
     rows = kx_ref.shape[1]
@@ -385,7 +387,7 @@
     count = rows - EARLY
     sends = [pltpu.make_async_copy(front, image.at[:, :EIGHT, :], sems.at[0])]
     sends[0].start()
-    pile(stack, 0, *(x[EARLY - 1] for x in inner))
+    pile(stack, 0, *(x[EARLY - 2] for x in inner))
     for n in range(count - 2):
         pile(stack, 1 + n, *(x[n] for x in last))
     pile(stack, count - 1, *(x[modes : 2 * modes] for x in rims))

time: 36.1 us -> 36.1 us (level)
    ppermute x6, waiting for transfers between devices: 5.97 us -> 4.66 us  [swapped(): return lax.ppermute(x, 'mode', pairs + [(j, i) for i, j in pairs])]
    ppermute x1, waiting for transfers between devices: 3.68 us -> 4.98 us  [swapped_between(): return lax.ppermute(x, 'space', pairs + [(j, i) for i, j in pairs])]
  transfers between devices with their start and end apart: 9 -> 9, of which waited for: 3 -> 2; matrix products, arithmetic and copies ran while one was open for 0% -> 0% of each run, Pallas kernels for 13% -> 13%
where the time goes in v5:
time: 36.1 us; the launch traced here: 36 us
  starting transfers between devices  17.8 us (49%)
  waiting for transfers between devices  9.65 us (27%)
  Pallas kernels  8.4 us (23%)
    ppermute x1, starting transfers between devices, swapped_between(): return lax.ppermute(x, 'space', pairs + [(j, i) for i, j in pairs])  7.08 us
    ppermute x6, starting transfers between devices, swapped(): return lax.ppermute(x, 'mode', pairs + [(j, i) for i, j in pairs])  5.63 us
    ppermute x2, starting transfers between devices, swapped_inside(): return lax.ppermute(x, 'space', pairs + [(j, i) for i, j in pairs])  5.05 us
    ppermute x1, waiting for transfers between devices, swapped_between(): return lax.ppermute(x, 'space', pairs + [(j, i) for i, j in pairs])  4.98 us
    ppermute x6, waiting for transfers between devices, swapped(): return lax.ppermute(x, 'mode', pairs + [(j, i) for i, j in pairs])  4.66 us
    pallas_call x1, Pallas kernels, early_image(): pl.pallas_call(early_body, out_shape=(jax.ShapeDtypeStruct((modes, EIGHT,...  3.72 us
    pallas_call x1, Pallas kernels, late_image(): pl.pallas_call(late_body, out_shape=jax.ShapeDtypeStruct((modes, rows, co...  2.05 us
    pallas_call x1, Pallas kernels, split_rows(): pl.pallas_call(split_body, out_shape=(jax.ShapeDtypeStruct((3 * modes + e...  1.54 us
  transfers between devices with their start and end apart: 9, of which 2 were waited for; matrix products, arithmetic and copies ran while one was open for 0% of the time, Pallas kernels for 13%

profile of v5, /device:TPU:121, one launch (start us, length us, event | category | flops | bytes accessed | tf_op | source)
XLA Modules:
  0.0 36.0 jit_solution(1930755341176062687)
XLA Ops:
  0.0 1.5 %shard_map.55 = (bf16[104,1024]{1,0:T(8,128)(2,1)S(1)}, bf16[10,32,1024]{2,1,0:T(8,128)(2,1)S(1)}, bf16[3,32,1024]{2,1,0:T(8,128)(2,1)S(1)}, bf16[16,1024]{1,0:T(8,128)(2,1)S(1)}) custom-call(bf16[32,16,1024]{2,1,0:T(8,128)(2,1)} %field_hbm.1, bf16[2,8,32,32]{3,2,1,0:T(8,128)(2,1)} %coupling_ref.1, s32[2,8,32,32]{3,2,1,0:T(8,128)} %pattern_ref.1, ...), custom_call_target="tpu_custom_call" | custom-call | bytes 2097152 | tf_op jit(solution)/shard_map/pallas_call | solution.py:106
  1.6 2.1 %collective-permute-start.1 = (bf16[104,1024]{1,0:T(8,128)(2,1)S(1)}, bf16[104,1024]{1,0:T(8,128)(2,1)S(1)}, u32[]{:S(2)}, u32[]{:S(2)}) collective-permute-start(bf16[104,1024]{1,0:T(8,128)(2,1)S(1)} %get-tuple-element.17.own.refs_0_), channel_id=1, source_target_pairs={{32,64},{96,128},{160,192},{224,0},{64,32},{128,96},{192,160},{0,2... | collective-permute-start | bytes 638984 | tf_op jit(solution)/shard_map/ppermute | solution.py:27
  3.7 0.4 %collective-permute-start = (bf16[104,1024]{1,0:T(8,128)(2,1)S(1)}, bf16[104,1024]{1,0:T(8,128)(2,1)S(1)}, u32[]{:S(2)}, u32[]{:S(2)}) collective-permute-start(bf16[104,1024]{1,0:T(8,128)(2,1)S(1)} %get-tuple-element.17.own.refs_0_), channel_id=1, source_target_pairs={{0,32},{64,96},{128,160},{192,224},{32,0},{96,64},{160,128},{224,1... | collective-permute-start | bytes 638984 | tf_op jit(solution)/shard_map/ppermute | solution.py:27
  4.1 1.2 %collective-permute-start.3 = (bf16[10,32,1024]{2,1,0:T(8,128)(2,1)S(1)}, bf16[10,32,1024]{2,1,0:T(8,128)(2,1)S(1)}, u32[]{:S(2)}, u32[]{:S(2)}) collective-permute-start(bf16[10,32,1024]{2,1,0:T(8,128)(2,1)S(1)} %get-tuple-element.18.refs_3_), channel_id=1, source_target_pairs={{32,64},{96,128},{160,192},{224,0},{64,32},{128,96},{192,160},{0,2... | collective-permute-start | bytes 1966088 | tf_op jit(solution)/shard_map/ppermute | solution.py:27
  5.2 0.0 collective-permute-start.2
  5.2 4.6 %collective-permute-done.1.odd.refs_2_ = bf16[104,1024]{1,0:T(8,128)(2,1)S(1)} collective-permute-done((bf16[104,1024]{1,0:T(8,128)(2,1)S(1)}, bf16[104,1024]{1,0:T(8,128)(2,1)S(1)}, u32[]{:S(2)}, u32[]{:S(2)}) %collective-permute-start.1) | collective-permute-done | bytes 213024 | tf_op jit(solution)/shard_map/ppermute | solution.py:27
  9.9 0.0 collective-permute-done.even.refs_1_
  9.9 0.0 copy-start.1
  9.9 0.0 copy-start.3
  9.9 0.0 copy-start
  9.9 0.0 copy-start.2
  10.0 0.8 %collective-permute-start.4 = (bf16[112,1024]{1,0:T(8,128)(2,1)S(1)}, bf16[112,1024]{1,0:T(8,128)(2,1)S(1)}, u32[]{:S(2)}, u32[]{:S(2)}) collective-permute-start(bf16[112,1024]{1,0:T(8,128)(2,1)S(1)} %get-tuple-element.21), channel_id=1, source_target_pairs={{1,2},{3,4},{5,6},{9,10},{11,12},{13,14},{17,18},{19,20},{21,22},{... | collective-permute-start | bytes 688136 | tf_op jit(solution)/shard_map/ppermute | solution.py:33
  10.8 4.2 %collective-permute-start.6 = (bf16[112,1024]{1,0:T(8,128)(2,1)S(1)}, bf16[112,1024]{1,0:T(8,128)(2,1)S(1)}, u32[]{:S(2)}, u32[]{:S(2)}) collective-permute-start(bf16[112,1024]{1,0:T(8,128)(2,1)S(1)} %get-tuple-element.23), channel_id=1, source_target_pairs={{0,1},{2,3},{4,5},{6,7},{8,9},{10,11},{12,13},{14,15},{16,17},{18,... | collective-permute-start | bytes 688136 | tf_op jit(solution)/shard_map/ppermute | solution.py:33
  15.0 0.0 copy-done.1
  15.0 0.0 copy-done.3
  15.0 0.3 shard_map.56.mix_ref
  15.3 0.3 shard_map.58
  15.6 7.1 %collective-permute-start.8 = (bf16[96,1024]{1,0:T(8,128)(2,1)S(1)}, bf16[96,1024]{1,0:T(8,128)(2,1)S(1)}, u32[]{:S(2)}, u32[]{:S(2)}) collective-permute-start(bf16[96,1024]{1,0:T(8,128)(2,1)S(1)} %shard_map.58), channel_id=1, source_target_pairs={{7,8},{15,16},{23,24},{8,7},{16,15},{24,23},{39,40},{47,48},{55,56... | collective-permute-start | bytes 589832 | tf_op jit(solution)/shard_map/ppermute | solution.py:38
  22.7 0.0 collective-permute-done.4.from_odd
  22.7 0.1 collective-permute-start.5
  22.8 0.0 collective-permute-done.6.from_even
  22.8 1.9 %collective-permute-start.7 = (bf16[3,32,1024]{2,1,0:T(8,128)(2,1)S(1)}, bf16[3,32,1024]{2,1,0:T(8,128)(2,1)S(1)}, u32[]{:S(2)}, u32[]{:S(2)}) collective-permute-start(bf16[3,32,1024]{2,1,0:T(8,128)(2,1)S(1)} %get-tuple-element.24.refs_6_), channel_id=1, source_target_pairs={{32,64},{96,128},{160,192},{224,0},{64,32},{128,96},{192,160},{0,2... | collective-permute-start | bytes 589832 | tf_op jit(solution)/shard_map/ppermute | solution.py:27
  24.7 0.0 collective-permute-done.3.refs_5_
  24.7 0.0 collective-permute-done.2.refs_4_
  24.7 0.0 copy-done
  24.7 0.0 copy-done.2
  24.7 3.7 %shard_map.59 = (f32[32,8,1024]{2,1,0:T(8,128)S(1)}, f32[6,32,1024]{2,1,0:T(8,128)S(1)}) custom-call(bf16[256,256]{1,0:T(8,128)(2,1)S(1)} %shard_map.56.mix_ref, f32[8,16,1024]{2,1,0:T(8,128)S(1)} %copy-done, f32[8,16,1024]{2,1,0:T(8,128)S(1)} %copy-done.2, bf16[104,1024]{1,0:T(8,128)(2,1)S(1)} %get-tuple-element.17.own.refs_0_, ...), custom_call_target="tpu_custom_call" | custom-call | flops 2952790016 | bytes 4194304 | tf_op jit(solution)/shard_map/pallas_call | solution.py:266
  28.4 5.0 %collective-permute-done.8.between = bf16[96,1024]{1,0:T(8,128)(2,1)S(1)} collective-permute-done((bf16[96,1024]{1,0:T(8,128)(2,1)S(1)}, bf16[96,1024]{1,0:T(8,128)(2,1)S(1)}, u32[]{:S(2)}, u32[]{:S(2)}) %collective-permute-start.8) | collective-permute-done | bytes 196640 | tf_op jit(solution)/shard_map/ppermute | solution.py:38
  33.4 0.5 %shard_map.60 = (f32[32,8,1024]{2,1,0:T(8,128)S(1)}, f32[32,1024]{1,0:T(8,128)S(1)}) custom-call(bf16[256,256]{1,0:T(8,128)(2,1)S(1)} %shard_map.56.mix_ref, f32[8,16,1024]{2,1,0:T(8,128)S(1)} %copy-done, bf16[112,1024]{1,0:T(8,128)(2,1)S(1)} %collective-permute-done.6.from_even, ...), custom_call_target="tpu_custom_call", output_to_operand_aliasing={{0}: (8, {})} | custom-call | flops 268435456 | bytes 1048576 | tf_op jit(solution)/shard_map/pallas_call | solution.py:362
  33.9 0.0 collective-permute-done.5.refs_7_
  33.9 0.0 collective-permute-done.7.refs_8_
  33.9 2.0 %shard_map.61 = f32[32,16,1024]{2,1,0:T(8,128)} custom-call(bf16[256,256]{1,0:T(8,128)(2,1)S(1)} %shard_map.56.mix_ref, f32[8,16,1024]{2,1,0:T(8,128)S(1)} %copy-done, f32[8,16,1024]{2,1,0:T(8,128)S(1)} %copy-done.2, bf16[104,1024]{1,0:T(8,128)(2,1)S(1)} %get-tuple-element.17.own.refs_0_, bf16[104,1024]{1,0:T(8,128)(2,1)S(1)} %collective-permute-done.even.refs_1_, ...), custom_call_target="tpu_custom_call" | custom-call | flops 1342177280 | bytes 4194304 | tf_op jit(solution)/shard_map/pallas_call | solution.py:428
  (1 shorter events, 0.0 us)
Async XLA Ops:
  1.6 8.3 %collective-permute-start.1 = (bf16[104,1024]{1,0:T(8,128)(2,1)S(1)}, bf16[104,1024]{1,0:T(8,128)(2,1)S(1)}, u32[]{:S(2)}, u32[]{:S(2)}) collective-permute-start(bf16[104,1024]{1,0:T(8,128)(2,1)S(1)} %get-tuple-element.17.own.refs_0_), channel_id=1, source_target_pairs={{32,64},{96,128},{160,192},{224,0},{64,32},{128,96},{192,160},{0,2... | collective-permute-start | bytes 638984 | tf_op jit(solution)/shard_map/ppermute | solution.py:27
  3.7 6.2 %collective-permute-start = (bf16[104,1024]{1,0:T(8,128)(2,1)S(1)}, bf16[104,1024]{1,0:T(8,128)(2,1)S(1)}, u32[]{:S(2)}, u32[]{:S(2)}) collective-permute-start(bf16[104,1024]{1,0:T(8,128)(2,1)S(1)} %get-tuple-element.17.own.refs_0_), channel_id=1, source_target_pairs={{0,32},{64,96},{128,160},{192,224},{32,0},{96,64},{160,128},{224,1... | collective-permute-start | bytes 638984 | tf_op jit(solution)/shard_map/ppermute | solution.py:27
  4.1 20.6 %collective-permute-start.3 = (bf16[10,32,1024]{2,1,0:T(8,128)(2,1)S(1)}, bf16[10,32,1024]{2,1,0:T(8,128)(2,1)S(1)}, u32[]{:S(2)}, u32[]{:S(2)}) collective-permute-start(bf16[10,32,1024]{2,1,0:T(8,128)(2,1)S(1)} %get-tuple-element.18.refs_3_), channel_id=1, source_target_pairs={{32,64},{96,128},{160,192},{224,0},{64,32},{128,96},{192,160},{0,2... | collective-permute-start | bytes 1966088 | tf_op jit(solution)/shard_map/ppermute | solution.py:27
  5.2 19.5 %collective-permute-start.2 = (bf16[10,32,1024]{2,1,0:T(8,128)(2,1)S(1)}, bf16[10,32,1024]{2,1,0:T(8,128)(2,1)S(1)}, u32[]{:S(2)}, u32[]{:S(2)}) collective-permute-start(bf16[10,32,1024]{2,1,0:T(8,128)(2,1)S(1)} %get-tuple-element.18.refs_3_), channel_id=1, source_target_pairs={{0,32},{64,96},{128,160},{192,224},{32,0},{96,64},{160,128},{224,1... | collective-permute-start | bytes 1966088 | tf_op jit(solution)/shard_map/ppermute | solution.py:27
  9.9 5.1 %copy-start.1 = (s32[2,8,32,32]{3,2,1,0:T(8,128)S(1)}, s32[2,8,32,32]{3,2,1,0:T(8,128)}, u32[]{:S(2)}) copy-start(s32[2,8,32,32]{3,2,1,0:T(8,128)} %pattern_ref.1) | copy-start | bytes 196612
  9.9 5.1 %copy-start.3 = (bf16[2,8,32,32]{3,2,1,0:T(8,128)(2,1)S(1)}, bf16[2,8,32,32]{3,2,1,0:T(8,128)(2,1)}, u32[]{:S(2)}) copy-start(bf16[2,8,32,32]{3,2,1,0:T(8,128)(2,1)} %coupling_ref.1) | copy-start | bytes 98308
  9.9 14.8 %copy-start = (f32[8,16,1024]{2,1,0:T(8,128)S(1)}, f32[8,16,1024]{2,1,0:T(8,128)}, u32[]{:S(2)}) copy-start(f32[8,16,1024]{2,1,0:T(8,128)} %kx_ref.5) | copy-start | bytes 1572868
  9.9 14.8 %copy-start.2 = (f32[8,16,1024]{2,1,0:T(8,128)S(1)}, f32[8,16,1024]{2,1,0:T(8,128)}, u32[]{:S(2)}) copy-start(f32[8,16,1024]{2,1,0:T(8,128)} %ky_ref.3) | copy-start | bytes 1572868
  10.0 12.7 %collective-permute-start.4 = (bf16[112,1024]{1,0:T(8,128)(2,1)S(1)}, bf16[112,1024]{1,0:T(8,128)(2,1)S(1)}, u32[]{:S(2)}, u32[]{:S(2)}) collective-permute-start(bf16[112,1024]{1,0:T(8,128)(2,1)S(1)} %get-tuple-element.21), channel_id=1, source_target_pairs={{1,2},{3,4},{5,6},{9,10},{11,12},{13,14},{17,18},{19,20},{21,22},{... | collective-permute-start | bytes 688136 | tf_op jit(solution)/shard_map/ppermute | solution.py:33
  10.8 12.0 %collective-permute-start.6 = (bf16[112,1024]{1,0:T(8,128)(2,1)S(1)}, bf16[112,1024]{1,0:T(8,128)(2,1)S(1)}, u32[]{:S(2)}, u32[]{:S(2)}) collective-permute-start(bf16[112,1024]{1,0:T(8,128)(2,1)S(1)} %get-tuple-element.23), channel_id=1, source_target_pairs={{0,1},{2,3},{4,5},{6,7},{8,9},{10,11},{12,13},{14,15},{16,17},{18,... | collective-permute-start | bytes 688136 | tf_op jit(solution)/shard_map/ppermute | solution.py:33
  15.6 17.8 %collective-permute-start.8 = (bf16[96,1024]{1,0:T(8,128)(2,1)S(1)}, bf16[96,1024]{1,0:T(8,128)(2,1)S(1)}, u32[]{:S(2)}, u32[]{:S(2)}) collective-permute-start(bf16[96,1024]{1,0:T(8,128)(2,1)S(1)} %shard_map.58), channel_id=1, source_target_pairs={{7,8},{15,16},{23,24},{8,7},{16,15},{24,23},{39,40},{47,48},{55,56... | collective-permute-start | bytes 589832 | tf_op jit(solution)/shard_map/ppermute | solution.py:38
  22.7 11.2 %collective-permute-start.5 = (bf16[3,32,1024]{2,1,0:T(8,128)(2,1)S(1)}, bf16[3,32,1024]{2,1,0:T(8,128)(2,1)S(1)}, u32[]{:S(2)}, u32[]{:S(2)}) collective-permute-start(bf16[3,32,1024]{2,1,0:T(8,128)(2,1)S(1)} %get-tuple-element.24.refs_6_), channel_id=1, source_target_pairs={{0,32},{64,96},{128,160},{192,224},{32,0},{96,64},{160,128},{224,1... | collective-permute-start | bytes 589832 | tf_op jit(solution)/shard_map/ppermute | solution.py:27
  22.8 11.1 %collective-permute-start.7 = (bf16[3,32,1024]{2,1,0:T(8,128)(2,1)S(1)}, bf16[3,32,1024]{2,1,0:T(8,128)(2,1)S(1)}, u32[]{:S(2)}, u32[]{:S(2)}) collective-permute-start(bf16[3,32,1024]{2,1,0:T(8,128)(2,1)S(1)} %get-tuple-element.24.refs_6_), channel_id=1, source_target_pairs={{32,64},{96,128},{160,192},{224,0},{64,32},{128,96},{192,160},{0,2... | collective-permute-start | bytes 589832 | tf_op jit(solution)/shard_map/ppermute | solution.py:27
